TPU v7x, 768 devices: a whole 4x8x12 slice. The times are simulated.
768 devices in a mesh: gx: 24 (over z, core), gy: 4 (over x), gz: 8 (over y).
Axes of the slice: x: 4, y: 8, z: 12, core: 2. Of those that a mesh axis runs over, the one named last changes fastest.
Arguments:
- loads: bfloat16 [24, 4, 8, 1024, 256], P('gx', 'gy', 'gz'), may hold values from -6 to 6
- start: bfloat16 [24, 4, 8, 1024, 256], P('gx', 'gy', 'gz'), may hold values from -6 to 6
- interface_op: bfloat16 [24, 4, 8, 1024, 1024], P('gx', 'gy', 'gz'), as said below
- block_order: int32 [24, 4, 8, 8], P('gx', 'gy', 'gz'), may hold values from 0 to 7, each once within a row
- interface_weights: float32 [24, 4, 8, 1024], P('gx', 'gy', 'gz'), may hold values from 0.1 to 0.3
- coarse_modes: float32 [24, 4, 8, 32, 1024], P('gx', 'gy', 'gz'), as said below
- region_weights: float32 [24, 4, 8, 32, 16], P('gx', 'gy', 'gz'), as said below
- region_inverse: float32 [24, 1024, 1024], P('gx', ('gy', 'gz')), as said below
- root_inverse: float32 [384, 384], P('gx'), as said below
Outputs:
- solution: float32 [24, 4, 8, 1024, 256], P('gx', 'gy', 'gz')
Inputs may be any that keep to these rules, and one draw needn't show every extreme that they name: `block_order`: each row lists every number from 0 to 7 once. `interface_op`: each subdomain's matrix has a dominant positive diagonal and full dense off-diagonal part. `region_inverse`: dense, with a dominant positive diagonal. `root_inverse`: dense, with a dominant positive diagonal. `coarse_modes`: dense. `region_weights`: dense.
All inputs are finite; a program needn't handle non-finite values.
Results may differ from a plain program's by a relative error of at most 0.0003.
Values sent between devices are 32-bit elements; how exact they have to be, the bound alone decides.
A program may use at most 32 MiB of HBM per device.

v0:
```python
import jax
import jax.numpy as jnp
from jax import lax
from jax.sharding import PartitionSpec as P

ITERS = 2


HIGH = lax.Precision.HIGHEST


def with_halo(cells, sides, width):
    for axis, dim in sides:
        count = lax.axis_size(axis)
        ends = count - 1
        head = lax.slice_in_dim(cells, 0, width, axis=dim)
        tail = lax.slice_in_dim(cells, cells.shape[dim] - width, cells.shape[dim], axis=dim)
        cells = jnp.concatenate(
            [
                lax.ppermute(tail, axis, [(i, (i + 1) % count) for i in range(ends)]),
                cells,
                lax.ppermute(head, axis, [((i + 1) % count, i) for i in range(ends)]),
            ],
            axis=dim,
        )
    return cells


def joined_along(parts, dim):
    lengths = list(parts.shape[1:])
    lengths[dim] *= parts.shape[0]
    return jnp.moveaxis(parts, 0, dim).reshape(lengths)


def sent_to_all(shard, axis):
    copies = jnp.broadcast_to(shard, (lax.axis_size(axis), *shard.shape))
    return lax.all_to_all(copies, axis, split_axis=0, concat_axis=0, tiled=True)


def gathered_copies(shard, axis, dim):
    return joined_along(sent_to_all(shard, axis), dim)


def sent_together(arrays, axis, dim, along):
    ends, at = ([], 0)
    for a in arrays[:-1]:
        at += a.shape[along]
        ends.append(at)
    both = jnp.concatenate(arrays, axis=along)
    return tuple(jnp.split(gathered_copies(both, axis, dim), ends, axis=along))


def transpose_dot(left, right):
    return lax.dot_general(
        left, right, (((0,), (0,)), ((), ())), precision=HIGH, preferred_element_type=jnp.float32
    )


def per_device(
    loads,
    start,
    interface_op,
    block_order,
    interface_weights,
    coarse_modes,
    region_weights,
    region_inverse,
    root_inverse,
):
    iface = interface_op.shape[-1]
    cases = loads.shape[-1]
    block = iface // 8
    matrix = interface_op.reshape(iface, iface)
    perm = block_order.reshape(8)
    weights = interface_weights.reshape(iface, 1)
    modes = coarse_modes.reshape(coarse_modes.shape[-2], iface)
    mode_count = modes.shape[0]
    root_map = region_weights.reshape(mode_count, region_weights.shape[-1])
    region_rows = region_inverse.reshape(mode_count, region_inverse.shape[-1])
    target = loads.reshape(iface, cases).astype(jnp.float32)
    solution = start.reshape(iface, cases).astype(jnp.float32)
    for step in range(ITERS):
        blocks = solution.astype(jnp.bfloat16).reshape(8, block, cases)
        local_iter = blocks[perm].reshape(iface, cases)
        result = jnp.dot(matrix, local_iter, preferred_element_type=jnp.float32).reshape(
            8, block, cases
        )
        product = jnp.zeros_like(result).at[perm].set(result)
        padded_x = with_halo(product[0:2], (("gx", 0),), 1)
        padded_y = with_halo(product[2:4], (("gy", 0),), 1)
        padded_z = with_halo(product[4:6], (("gz", 0),), 1)
        assembled = jnp.concatenate(
            [
                (product[0] + padded_x[0])[None],
                (product[1] + padded_x[3])[None],
                (product[2] + padded_y[0])[None],
                (product[3] + padded_y[3])[None],
                (product[4] + padded_z[0])[None],
                (product[5] + padded_z[3])[None],
                product[6:],
            ],
            axis=0,
        ).reshape(iface, cases)
        residual = target - assembled
        coarse = jnp.dot(modes, residual, precision=HIGH, preferred_element_type=jnp.float32)
        coeff_piece, weight_piece = sent_together((coarse, root_map), ("gy", "gz"), 0, 1)
        region_part = jnp.dot(
            region_rows, coeff_piece, precision=HIGH, preferred_element_type=jnp.float32
        )
        root_input = transpose_dot(weight_piece, coeff_piece)
        root_part = jnp.dot(
            root_inverse,
            gathered_copies(root_input, "gx", 0),
            precision=HIGH,
            preferred_element_type=jnp.float32,
        )
        amplitude = region_part + jnp.dot(
            root_map, root_part, precision=HIGH, preferred_element_type=jnp.float32
        )
        solution = solution + weights * residual + transpose_dot(modes, amplitude)
    return solution.reshape(1, 1, 1, iface, cases)


def solution(mesh):
    placed = (
        P("gx", "gy", "gz", None, None),
        P("gx", "gy", "gz", None, None),
        P("gx", "gy", "gz", None, None),
        P("gx", "gy", "gz", None),
        P("gx", "gy", "gz", None),
        P("gx", "gy", "gz", None, None),
        P("gx", "gy", "gz", None, None),
        P("gx", ("gy", "gz"), None),
        P("gx", None),
    )
    return jax.shard_map(
        per_device,
        mesh=mesh,
        in_specs=placed,
        out_specs=P("gx", "gy", "gz", None, None),
        check_vma=False,
    )
```

profile of v0, /device:TPU:1, one launch (start us, length us, event | category | flops | bytes accessed | tf_op | source)
XLA Modules:
  0.0 251.2 jit_solution(17657972980683409807)
XLA Ops:
  0.0 0.8 fusion.34
  0.8 2.4 gather_fusion
  3.3 1.8 fusion.4
  5.1 1.3 copy.25
  6.5 2.0 scatter_fusion
  8.5 5.4 %collective-permute-start = (f32[1,128,256]{2,1,0:T(8,128)S(1)}, f32[1,128,256]{2,1,0:T(8,128)S(1)}, u32[]{:S(2)}, u32[]{:S(2)}) collective-permute-start(f32[1,128,256]{2,1,0:T(8,128)S(1)} %slice.91), channel_id=1, source_target_pairs={{0,32},{32,64},{64,96},{96,128},{128,160},{160,192},{192,224},{224... | collective-permute-start | bytes 393224 | tf_op jit(solution)/shard_map/ppermute | solution.py:20
  13.9 7.2 %collective-permute-done = f32[1,128,256]{2,1,0:T(8,128)S(1)} collective-permute-done((f32[1,128,256]{2,1,0:T(8,128)S(1)}, f32[1,128,256]{2,1,0:T(8,128)S(1)}, u32[]{:S(2)}, u32[]{:S(2)}) %collective-permute-start) | collective-permute-done | bytes 131104 | tf_op jit(solution)/shard_map/ppermute | solution.py:20
  21.1 0.8 fusion.36
  21.8 2.0 collective-permute-start.1
  23.9 2.0 copy.15
  25.9 2.2 copy.30
  28.2 0.8 copy.19
  28.9 1.4 collective-permute-start.2
  30.3 1.3 collective-permute-start.3
  31.6 1.3 collective-permute-start.4
  33.0 1.3 collective-permute-start.5
  34.3 1.6 add_dynamic-update-slice_fusion.10
  35.8 0.7 add_dynamic-update-slice_fusion.9
  36.5 1.1 collective-permute-done.3
  37.6 0.7 add_dynamic-update-slice_fusion.8
  38.3 0.7 add_dynamic-update-slice_fusion.7
  39.0 1.1 collective-permute-done.5
  40.0 0.7 add_dynamic-update-slice_fusion.6
  40.7 0.7 slice_dynamic-update-slice_fusion.1
  41.5 1.4 sub.29
  42.9 0.7 convolution_bitcast_fusion.3
  43.7 47.1 %all_to_all.20 = f32[32,32,272]{2,1,0:T(8,128)S(1)} all-to-all(f32[32,32,272]{2,1,0:T(8,128)S(1)} %broadcast_in_dim.8), channel_id=1, replica_groups=mesh['gx'=24,'gy'=4,'gz'=8] {'gy','gz'}, dimensions={0} | all-to-all | bytes 2228224 | tf_op jit(solution)/shard_map/all_to_all | solution.py:37
  90.8 1.2 copy-done.1
  92.0 1.0 fusion.20
  93.0 0.8 broadcast_in_dim.9
  93.8 18.2 %all-to-all-start.1 = ((f32[24,16,256]{2,1,0:T(8,128)}), f32[24,16,256]{2,1,0:T(8,128)}, u32[]{:S(2)}, u32[]{:S(2)}) async-start(f32[24,16,256]{2,1,0:T(8,128)} %broadcast_in_dim.9), calls=%async_computation.1 | async-start | bytes 786432 | tf_op jit(solution)/shard_map/all_to_all | solution.py:37
  112.0 2.1 copy.14
  114.1 1.3 copy.26
  115.5 3.1 %fusion.22 = f32[256,32]{1,0:T(8,128)S(1)} fusion(f32[1024,272]{1,0:T(8,128)} %bitcast.101, f32[1,32,1024]{2,1,0:T(8,128)S(1)} %copy-done.12), kind=kOutput, calls=%fused_computation.31 | convolution fusion | flops 100663296 | bytes 1212416 | tf_op jit(solution)/shard_map/dot_general | solution.py:107
  118.6 11.8 %all-to-all-done.1 = f32[24,16,256]{2,1,0:T(8,128)} async-done(((f32[24,16,256]{2,1,0:T(8,128)}), f32[24,16,256]{2,1,0:T(8,128)}, u32[]{:S(2)}, u32[]{:S(2)}) %all-to-all-start.1) | async-done | bytes 393248 | tf_op jit(solution)/shard_map/all_to_all | solution.py:37
  130.4 1.8 fusion.38
  132.2 0.9 convolution_add_fusion.1
  133.2 3.5 %fusion.37 = (bf16[1024,256]{0,1:T(8,128)(2,1)}, f32[1024,256]{0,1:T(8,128)}) fusion(f32[256,32]{1,0:T(8,128)S(1)} %convolution_add_fusion.1, f32[1,1,1,32,1024]{4,3,2,1,0:T(8,128)S(1)} %copy-done.10, f32[1024,256]{0,1:T(8,128)} %copy.26, bf16[1,1,1,1024,256]{3,4,2,1,0:T(8,128)(2,1)S(1)} %copy-done.5, f32[1024]{0:T(1024)} %bitcast.118, ...), kind=kOutput, calls=%fused_computation.64 | convolution fusion | flops 102498304 | bytes 3837952 | tf_op jit(solution)/shard_map/dot_general | solution.py:54
  136.6 1.2 copy.27
  137.9 1.5 gather_fusion.1
  139.4 1.8 fusion.7
  141.2 1.3 copy.28
  142.6 2.0 scatter_fusion.1
  144.6 2.3 collective-permute-start.6
  146.9 2.4 collective-permute-done.6
  149.4 2.2 collective-permute-start.7
  151.6 1.3 collective-permute-start.8
  152.9 1.3 collective-permute-start.9
  154.2 4.3 %collective-permute-start.10 = (f32[1,128,256]{2,1,0:T(8,128)S(1)}, f32[1,128,256]{2,1,0:T(8,128)S(1)}, u32[]{:S(2)}, u32[]{:S(2)}) collective-permute-start(f32[1,128,256]{2,1,0:T(8,128)S(1)} %get-tuple-element.7), channel_id=1, source_target_pairs={{0,1},{1,2},{2,3},{3,4},{4,5},{5,6},{6,7},{8,9},{9,10},{10,11},{11... | collective-permute-start | bytes 393224 | tf_op jit(solution)/shard_map/ppermute | solution.py:20
  158.5 1.3 collective-permute-start.11
  160.3 1.4 collective-permute-done.10
  161.7 3.8 %collective-permute-done.11 = f32[1,128,256]{2,1,0:T(8,128)S(1)} collective-permute-done((f32[1,128,256]{2,1,0:T(8,128)S(1)}, f32[1,128,256]{2,1,0:T(8,128)S(1)}, u32[]{:S(2)}, u32[]{:S(2)}) %collective-permute-start.11) | collective-permute-done | bytes 131104 | tf_op jit(solution)/shard_map/ppermute | solution.py:22
  165.7 0.8 copy-done.8
  167.4 42.0 %all_to_all.21 = f32[32,32,272]{2,1,0:T(8,128)S(1)} all-to-all(f32[32,32,272]{2,1,0:T(8,128)S(1)} %broadcast_in_dim.10), channel_id=1, replica_groups=mesh['gx'=24,'gy'=4,'gz'=8] {'gy','gz'}, dimensions={0} | all-to-all | bytes 2228224 | tf_op jit(solution)/shard_map/all_to_all | solution.py:37
  209.4 1.2 copy-done.2
  210.6 1.0 fusion.16
  211.6 0.8 broadcast_in_dim.11
  212.4 12.3 %all-to-all-start.3 = ((f32[24,16,256]{2,1,0:T(8,128)}), f32[24,16,256]{2,1,0:T(8,128)}, u32[]{:S(2)}, u32[]{:S(2)}) async-start(f32[24,16,256]{2,1,0:T(8,128)} %broadcast_in_dim.11), calls=%async_computation.3 | async-start | bytes 786432 | tf_op jit(solution)/shard_map/all_to_all | solution.py:37
  224.7 1.3 copy.29
  226.0 3.1 %fusion.18 = f32[256,32]{1,0:T(8,128)S(1)} fusion(f32[1024,272]{1,0:T(8,128)} %bitcast.103, f32[1,32,1024]{2,1,0:T(8,128)S(1)} %copy-done.12), kind=kOutput, calls=%fused_computation.27 | convolution fusion | flops 100663296 | bytes 1212416 | tf_op jit(solution)/shard_map/dot_general | solution.py:107
  229.1 13.9 %all-to-all-done.3 = f32[24,16,256]{2,1,0:T(8,128)} async-done(((f32[24,16,256]{2,1,0:T(8,128)}), f32[24,16,256]{2,1,0:T(8,128)}, u32[]{:S(2)}, u32[]{:S(2)}) %all-to-all-start.3) | async-done | bytes 393248 | tf_op jit(solution)/shard_map/all_to_all | solution.py:37
  243.0 1.8 fusion.39
  245.1 3.6 %fusion.11 = f32[1,1,1,1024,256]{3,4,2,1,0:T(8,128)} fusion(f32[256,32]{1,0:T(8,128)S(1)} %convolution_add_fusion, f32[1024,256]{0,1:T(8,128)} %get-tuple-element.18, f32[1024,256]{0,1:T(8,128)} %copy.29, bf16[1,1,1,1024,256]{3,4,2,1,0:T(8,128)(2,1)S(1)} %copy-done.6, f32[1024]{0:T(1024)S(1)} %bitcast.119, f32[1,1,1,32,1024]{4,3,2,1,0:T(8,128)S(1)} %copy-done.10), kind=kOutput, calls=%fused_computation.12 | convolution fusion | flops 101974016 | bytes 3837952 | tf_op jit(solution)/shard_map/dot_general | solution.py:54
  248.7 2.5 %copy.24 = f32[1,1,1,1024,256]{4,3,2,1,0:T(8,128)} copy(f32[1,1,1,1024,256]{3,4,2,1,0:T(8,128)} %fusion.11) | data formatting | bytes 2097152 | tf_op jit(solution)/shard_map/reshape | solution.py:121
  (60 shorter events, 2.2 us)
Async XLA Ops:
  0.0 3.3 %copy-start = (bf16[1,1,1,1024,1024]{4,3,2,1,0:T(8,128)(2,1)S(1)}, bf16[1,1,1,1024,1024]{4,3,2,1,0:T(8,128)(2,1)}, u32[]{:S(2)}) copy-start(bf16[1,1,1,1024,1024]{4,3,2,1,0:T(8,128)(2,1)} %param.11) | copy-start | bytes 6291460
  0.8 5.6 %copy-start.17 = (s32[8]{0:T(128)}, s32[8]{0:T(128)S(1)}, u32[]{:S(2)}) copy-start(s32[8]{0:T(128)S(1)} %fusion.34) | copy-start | bytes 100
  0.8 2.4 copy-start.16
  8.5 12.6 %collective-permute-start = (f32[1,128,256]{2,1,0:T(8,128)S(1)}, f32[1,128,256]{2,1,0:T(8,128)S(1)}, u32[]{:S(2)}, u32[]{:S(2)}) collective-permute-start(f32[1,128,256]{2,1,0:T(8,128)S(1)} %slice.91), channel_id=1, source_target_pairs={{0,32},{32,64},{64,96},{96,128},{128,160},{160,192},{192,224},{224... | collective-permute-start | bytes 393224 | tf_op jit(solution)/shard_map/ppermute | solution.py:20
  21.8 12.4 %collective-permute-start.1 = (f32[1,128,256]{2,1,0:T(8,128)}, f32[1,128,256]{2,1,0:T(8,128)}, u32[]{:S(2)}, u32[]{:S(2)}) collective-permute-start(f32[1,128,256]{2,1,0:T(8,128)} %get-tuple-element.16), channel_id=1, source_target_pairs={{32,0},{64,32},{96,64},{128,96},{160,128},{192,160},{224,192},{256... | collective-permute-start | bytes 393224 | tf_op jit(solution)/shard_map/ppermute | solution.py:22
  28.9 12.5 %copy-start.3 = (f32[1,1,1,1024,256]{4,3,2,1,0:T(8,128)S(1)}, f32[1,1,1,1024,256]{4,3,2,1,0:T(8,128)}, u32[]{:S(2)}) copy-start(f32[1,1,1,1024,256]{4,3,2,1,0:T(8,128)} %copy.30) | copy-start | bytes 3145732
  28.9 6.9 %collective-permute-start.2 = (f32[1,128,256]{2,1,0:T(8,128)}, f32[1,128,256]{2,1,0:T(8,128)S(1)}, u32[]{:S(2)}, u32[]{:S(2)}) collective-permute-start(f32[1,128,256]{2,1,0:T(8,128)} %get-tuple-element.14), channel_id=1, source_target_pairs={{0,8},{8,16},{16,24},{1,9},{9,17},{17,25},{2,10},{10,18},{18,26},{... | collective-permute-start | bytes 393224 | tf_op jit(solution)/shard_map/ppermute | solution.py:20
  30.3 7.3 %collective-permute-start.3 = (f32[1,128,256]{2,1,0:T(8,128)S(1)}, f32[1,128,256]{2,1,0:T(8,128)S(1)}, u32[]{:S(2)}, u32[]{:S(2)}) collective-permute-start(f32[1,128,256]{2,1,0:T(8,128)S(1)} %get-tuple-element.15), channel_id=1, source_target_pairs={{8,0},{16,8},{24,16},{9,1},{17,9},{25,17},{10,2},{18,10},{26,18},{... | collective-permute-start | bytes 393224 | tf_op jit(solution)/shard_map/ppermute | solution.py:22
  31.6 6.6 %collective-permute-start.4 = (f32[1,128,256]{2,1,0:T(8,128)S(1)}, f32[1,128,256]{2,1,0:T(8,128)S(1)}, u32[]{:S(2)}, u32[]{:S(2)}) collective-permute-start(f32[1,128,256]{2,1,0:T(8,128)S(1)} %get-tuple-element.13), channel_id=1, source_target_pairs={{0,1},{1,2},{2,3},{3,4},{4,5},{5,6},{6,7},{8,9},{9,10},{10,11},{11... | collective-permute-start | bytes 393224 | tf_op jit(solution)/shard_map/ppermute | solution.py:20
  33.0 7.1 %collective-permute-start.5 = (f32[1,128,256]{2,1,0:T(8,128)S(1)}, f32[1,128,256]{2,1,0:T(8,128)S(1)}, u32[]{:S(2)}, u32[]{:S(2)}) collective-permute-start(f32[1,128,256]{2,1,0:T(8,128)S(1)} %get-tuple-element.11), channel_id=1, source_target_pairs={{1,0},{2,1},{3,2},{4,3},{5,4},{6,5},{7,6},{9,8},{10,9},{11,10},{12... | collective-permute-start | bytes 393224 | tf_op jit(solution)/shard_map/ppermute | solution.py:22
  41.5 1.4 copy-start.10
  90.8 1.2 copy-start.1
  92.0 22.1 %copy-start.7 = (f32[8,128,256]{2,1,0:T(8,128)S(1)}, f32[8,128,256]{2,1,0:T(8,128)}, u32[]{:S(2)}) copy-start(f32[8,128,256]{2,1,0:T(8,128)} %slice_dynamic-update-slice_fusion.1) | copy-start | bytes 3145732
  93.8 36.6 %all-to-all-start.1 = ((f32[24,16,256]{2,1,0:T(8,128)}), f32[24,16,256]{2,1,0:T(8,128)}, u32[]{:S(2)}, u32[]{:S(2)}) async-start(f32[24,16,256]{2,1,0:T(8,128)} %broadcast_in_dim.9), calls=%async_computation.1 | async-start | bytes 786432 | tf_op jit(solution)/shard_map/all_to_all | solution.py:37
  112.0 3.4 %copy-start.12 = (f32[1,32,1024]{2,1,0:T(8,128)S(1)}, f32[1,32,1024]{2,1,0:T(8,128)}, u32[]{:S(2)}) copy-start(f32[1,32,1024]{2,1,0:T(8,128)} %param.16) | copy-start | bytes 393220
  115.5 17.7 %copy-start.5 = (bf16[1,1,1,1024,256]{3,4,2,1,0:T(8,128)(2,1)S(1)}, bf16[1,1,1,1024,256]{3,4,2,1,0:T(8,128)(2,1)}, u32[]{:S(2)}) copy-start(bf16[1,1,1,1024,256]{3,4,2,1,0:T(8,128)(2,1)} %copy.15) | copy-start | bytes 1572868
  115.5 17.7 %copy-start.11 = (bf16[1,1,1,1024,256]{3,4,2,1,0:T(8,128)(2,1)S(1)}, bf16[1,1,1,1024,256]{3,4,2,1,0:T(8,128)(2,1)}, u32[]{:S(2)}) copy-start(bf16[1,1,1,1024,256]{3,4,2,1,0:T(8,128)(2,1)} %copy.14) | copy-start | bytes 1572868
  141.2 1.4 copy-start.18
  144.6 4.7 %collective-permute-start.6 = (f32[1,128,256]{2,1,0:T(8,128)S(1)}, f32[1,128,256]{2,1,0:T(8,128)S(1)}, u32[]{:S(2)}, u32[]{:S(2)}) collective-permute-start(f32[1,128,256]{2,1,0:T(8,128)S(1)} %slice.98), channel_id=1, source_target_pairs={{0,32},{32,64},{64,96},{96,128},{128,160},{160,192},{192,224},{224... | collective-permute-start | bytes 393224 | tf_op jit(solution)/shard_map/ppermute | solution.py:20
  149.4 16.1 %copy-start.4 = (f32[1,1,1,1024,256]{4,3,2,1,0:T(8,128)S(1)}, f32[1,1,1,1024,256]{4,3,2,1,0:T(8,128)}, u32[]{:S(2)}) copy-start(f32[1,1,1,1024,256]{4,3,2,1,0:T(8,128)} %copy.30) | copy-start | bytes 3145732
  149.4 10.4 %collective-permute-start.7 = (f32[1,128,256]{2,1,0:T(8,128)S(1)}, f32[1,128,256]{2,1,0:T(8,128)S(1)}, u32[]{:S(2)}, u32[]{:S(2)}) collective-permute-start(f32[1,128,256]{2,1,0:T(8,128)S(1)} %get-tuple-element.10), channel_id=1, source_target_pairs={{32,0},{64,32},{96,64},{128,96},{160,128},{192,160},{224,192},{256... | collective-permute-start | bytes 393224 | tf_op jit(solution)/shard_map/ppermute | solution.py:22
  151.6 8.2 %collective-permute-start.8 = (f32[1,128,256]{2,1,0:T(8,128)S(1)}, f32[1,128,256]{2,1,0:T(8,128)S(1)}, u32[]{:S(2)}, u32[]{:S(2)}) collective-permute-start(f32[1,128,256]{2,1,0:T(8,128)S(1)} %get-tuple-element.8), channel_id=1, source_target_pairs={{0,8},{8,16},{16,24},{1,9},{9,17},{17,25},{2,10},{10,18},{18,26},{... | collective-permute-start | bytes 393224 | tf_op jit(solution)/shard_map/ppermute | solution.py:20
  152.9 7.3 %collective-permute-start.9 = (f32[1,128,256]{2,1,0:T(8,128)S(1)}, f32[1,128,256]{2,1,0:T(8,128)S(1)}, u32[]{:S(2)}, u32[]{:S(2)}) collective-permute-start(f32[1,128,256]{2,1,0:T(8,128)S(1)} %get-tuple-element.9), channel_id=1, source_target_pairs={{8,0},{16,8},{24,16},{9,1},{17,9},{25,17},{10,2},{18,10},{26,18},{... | collective-permute-start | bytes 393224 | tf_op jit(solution)/shard_map/ppermute | solution.py:22
  154.2 7.4 %collective-permute-start.10 = (f32[1,128,256]{2,1,0:T(8,128)S(1)}, f32[1,128,256]{2,1,0:T(8,128)S(1)}, u32[]{:S(2)}, u32[]{:S(2)}) collective-permute-start(f32[1,128,256]{2,1,0:T(8,128)S(1)} %get-tuple-element.7), channel_id=1, source_target_pairs={{0,1},{1,2},{2,3},{3,4},{4,5},{5,6},{6,7},{8,9},{9,10},{10,11},{11... | collective-permute-start | bytes 393224 | tf_op jit(solution)/shard_map/ppermute | solution.py:20
  158.5 7.0 %collective-permute-start.11 = (f32[1,128,256]{2,1,0:T(8,128)S(1)}, f32[1,128,256]{2,1,0:T(8,128)S(1)}, u32[]{:S(2)}, u32[]{:S(2)}) collective-permute-start(f32[1,128,256]{2,1,0:T(8,128)S(1)} %get-tuple-element.5), channel_id=1, source_target_pairs={{1,0},{2,1},{3,2},{4,3},{5,4},{6,5},{7,6},{9,8},{10,9},{11,10},{12... | collective-permute-start | bytes 393224 | tf_op jit(solution)/shard_map/ppermute | solution.py:22
  165.5 1.0 copy-start.8
  209.4 1.2 copy-start.2
  209.4 15.3 %copy-start.9 = (f32[8,128,256]{2,1,0:T(8,128)S(1)}, f32[8,128,256]{2,1,0:T(8,128)}, u32[]{:S(2)}) copy-start(f32[8,128,256]{2,1,0:T(8,128)} %copy-done.8) | copy-start | bytes 3145732
  212.4 30.6 %all-to-all-start.3 = ((f32[24,16,256]{2,1,0:T(8,128)}), f32[24,16,256]{2,1,0:T(8,128)}, u32[]{:S(2)}, u32[]{:S(2)}) async-start(f32[24,16,256]{2,1,0:T(8,128)} %broadcast_in_dim.11), calls=%async_computation.3 | async-start | bytes 786432 | tf_op jit(solution)/shard_map/all_to_all | solution.py:37
  224.7 18.3 %copy-start.13 = (f32[16,384]{1,0:T(8,128)S(1)}, f32[16,384]{1,0:T(8,128)}, u32[]{:S(2)}) copy-start(f32[16,384]{1,0:T(8,128)} %param.17) | copy-start | bytes 73732
  224.7 20.1 %copy-start.14 = (f32[1,1,1,32,16]{3,4,2,1,0:T(8,128)S(1)}, f32[1,1,1,32,16]{3,4,2,1,0:T(8,128)}, u32[]{:S(2)}) copy-start(f32[1,1,1,32,16]{3,4,2,1,0:T(8,128)} %param.15) | copy-start | bytes 6148
  226.0 19.1 %copy-start.6 = (bf16[1,1,1,1024,256]{3,4,2,1,0:T(8,128)(2,1)S(1)}, bf16[1,1,1,1024,256]{3,4,2,1,0:T(8,128)(2,1)}, u32[]{:S(2)}) copy-start(bf16[1,1,1,1024,256]{3,4,2,1,0:T(8,128)(2,1)} %copy.15) | copy-start | bytes 1572868
  226.0 19.1 %copy-start.15 = (f32[1,1,1,1024]{3,2,1,0:T(1,128)S(1)}, f32[1,1,1,1024]{3,2,1,0:T(1,128)}, u32[]{:S(2)}) copy-start(f32[1,1,1,1024]{3,2,1,0:T(1,128)} %param.13) | copy-start | bytes 12292
where the time goes:
time: 254 us; the launch traced here: 251 us
  blocking collectives  89.1 us (35%)
  starting transfers between devices  55.9 us (22%)
  waiting for transfers between devices  43.1 us (17%)
  local copies, waits for them, and re-layouts  30.2 us (12%)
  matrix products  24.9 us (10%)
  other arithmetic  7.53 us (3%)
    all_to_all x2, blocking collectives, sent_to_all(): return lax.all_to_all(copies, axis, split_axis=0, concat_axis=0, tiled=True)  89.1 us
    all_to_all x2, starting transfers between devices, sent_to_all(): return lax.all_to_all(copies, axis, split_axis=0, concat_axis=0, tiled=True)  30.5 us
    all_to_all x2, waiting for transfers between devices, sent_to_all(): return lax.all_to_all(copies, axis, split_axis=0, concat_axis=0, tiled=True)  25.7 us
    ppermute x6, starting transfers between devices, with_halo(): lax.ppermute(tail, axis, [(i, (i + 1) % count) for i in range(ends)])  15.9 us
    ppermute x6, waiting for transfers between devices, with_halo(): lax.ppermute(tail, axis, [(i, (i + 1) % count) for i in range(ends)])  11 us
    ppermute x6, starting transfers between devices, with_halo(): lax.ppermute(head, axis, [((i + 1) % count, i) for i in range(ends)])  9.4 us
    dot_general x4, matrix products, transpose_dot(): lax.dot_general(left, right, (((0,), (0,)), ((), ())), precision=HIGH, pr...  9.03 us
    unnamed x41, local copies, waits for them, and re-layouts  8.14 us
  transfers between devices with their start and end apart: 14, of which 9 were waited for; matrix products, arithmetic and copies ran while one was open for 8% of the time, Pallas kernels for 0%

commit v1 on v0

v1 whole, which is shorter than its diff:
```python
import functools

import jax
import jax.numpy as jnp
from jax import lax
from jax.experimental import pallas as pl
from jax.experimental.pallas import tpu as pltpu
from jax.sharding import PartitionSpec as P

ITERS = 2
MESH = pl.DeviceIdType.MESH
F32 = jnp.float32
BF16 = jnp.bfloat16
HIGH = lax.Precision.HIGHEST
PAIRS = ((2, 3), (4, 5), (0, 1), (6, 7))


def dot(a, b):
    return jnp.dot(a, b, preferred_element_type=F32)


def split3(x):
    high = x.astype(BF16)
    rest = x - high.astype(F32)
    mid = rest.astype(BF16)
    low = (rest - mid.astype(F32)).astype(BF16)
    return high, mid, low


def split_rows(x):
    return jnp.concatenate([t.astype(F32) for t in split3(x)], axis=0).astype(BF16)


def rows_dot(left, right):
    n = left.shape[0] // 3
    high, mid, low = split3(right)
    p = dot(left, high)
    q = dot(left[: 2 * n], mid)
    r = dot(left[:n], low)
    return ((r + q[n:]) + p[2 * n :]) + (q[:n] + p[n : 2 * n]) + p[:n]


def deep_left(x, depth):
    high, mid, low = (t.astype(F32) for t in split3(x))
    terms = [high, high, mid, high, mid, low]
    fill = depth - 6 * x.shape[0]
    if fill:
        terms.append(jnp.zeros((fill, x.shape[1]), F32))
    return jnp.concatenate(terms, axis=0).T.astype(BF16)


def deep_right(x, depth):
    high, mid, low = split3(x)
    terms = [high, mid, high, low, mid, high]
    fill = depth - 6 * x.shape[0]
    if fill:
        terms.append(jnp.zeros((fill, x.shape[1]), BF16))
    return jnp.concatenate(terms, axis=0)


def pad_to(n, m):
    return -(-n // m) * m


def kernel(
    nx, ny, nz,
    perm_s, loads_h, start_h, op_h, w_h, modes_h, rw_h, rinv_h, root_h,
    base_o, g_o, root_o,
    loads_v, start_v, op_v, w_v, modes_v, rw_v,
    local, prod, halo, sol, solb, res, wb, modes_s, modes_t, g_t,
    rblk, rblk_s, rinv2, rinv_s,
    t_all, c_all, s_all, rp_send, rp_all, z_all, p_send, p_recv, root_v,
    in_sem, hs, hr, ts, tr, cs, cr, ss, sr, zs, zr, rs, rr, ps, pr, ms, mr, xs, xr, out_sem,
):
    gx, gy, gz = lax.axis_index("gx"), lax.axis_index("gy"), lax.axis_index("gz")
    nchip = nx // 2
    chip, core = gx // 2, lax.rem(gx, 2)
    modes_n, iface = modes_v.shape
    block = iface // 8
    width = nz * modes_n
    mate = (gx + 1 - 2 * core, gy, gz)
    beside = (lax.rem(gx + 2 * core - 1 + nx, nx), gy, gz)

    def along_z(off):
        return (gx, gy, lax.rem(gz + off, nz))

    def along_y(off):
        return (gx, lax.rem(gy + off, ny), gz)

    def along_x(off):
        return (lax.rem(chip + off, nchip) * 2 + core, gy, gz)

    def far_first(n):
        return sorted(range(1, n), key=lambda o: -min(o, n - o))

    def remote(src, dst, send, recv, device):
        return pltpu.make_async_remote_copy(
            src_ref=src, dst_ref=dst, send_sem=send, recv_sem=recv,
            device_id=device, device_id_type=MESH,
        )

    def columns(a):
        return pl.ds(pl.multiple_of(a * width, 128), width)

    loaded = {}
    for i, (name, src, dst) in enumerate((
        ("start", start_h, start_v), ("op", op_h, op_v), ("modes", modes_h, modes_v), ("rw", rw_h, rw_v),
        ("loads", loads_h, loads_v), ("w", w_h, w_v), ("root", root_h, rinv2.at[0]),
        ("rinv", rinv_h.at[:, columns(gy)], rblk.at[gy]),
    )):
        loaded[name] = pltpu.make_async_copy(src, dst, in_sem.at[i])
        loaded[name].start()

    barrier = pltpu.get_barrier_semaphore()
    greeted = (
        [along_x(o) for o in far_first(nchip)] + [along_z(o) for o in far_first(nz)]
        + [along_y(o) for o in far_first(ny)] + [beside, mate]
    )
    for device in greeted:
        pl.semaphore_signal(barrier, inc=1, device_id=device, device_id_type=MESH)

    has = (gx > 0, gx < nx - 1, gy > 0, gy < ny - 1, gz > 0, gz < nz - 1)
    towards = (
        (lax.rem(gx + nx - 1, nx), gy, gz), (lax.rem(gx + 1, nx), gy, gz),
        along_y(ny - 1), along_y(1), along_z(nz - 1), along_z(1),
    )

    def halo_copy(it, f):
        return remote(
            prod.at[it, f], halo.at[it, f ^ 1], hs.at[it, f], hr.at[it, f ^ 1], towards[f]
        )

    for it in range(ITERS):
        for f in range(6):

            @pl.when(jnp.logical_not(has[f]))
            def _(it=it, f=f):
                halo[it, f] = jnp.zeros_like(halo[it, f])

    perm = [perm_s[j] for j in range(8)]
    inverse = []
    for f in range(8):
        at = jnp.int32(0)
        for j in range(8):
            at = jnp.where(perm[j] == f, j, at)
        inverse.append(at)

    def send_pair(it, pair):
        for f in pair:
            if f < 6:

                @pl.when(has[f])
                def _(it=it, f=f):
                    halo_copy(it, f).start()

    def t_copy(it, off):
        return remote(
            t_all.at[it, gz], t_all.at[it, gz], ts.at[it, off], tr.at[it, off], along_z(off)
        )

    def c_copy(it, off):
        return remote(
            c_all.at[it, gz], c_all.at[it, gz], cs.at[it, off], cr.at[it, off], along_z(off)
        )

    def s_copy(it, off):
        return remote(
            s_all.at[it, gy], s_all.at[it, gy], ss.at[it, off], sr.at[it, off], along_y(off)
        )

    def z_copy(it, off):
        return remote(
            z_all.at[it, gx], z_all.at[it, gx], zs.at[it, off], zr.at[it, off], along_x(off)
        )

    def r_copy(off):
        to = along_y(off)
        return remote(rinv_h.at[:, columns(to[1])], rblk.at[gy], rs.at[off], rr.at[off], to)

    def rp_copy(it, off):
        to = along_y(off)
        return remote(
            rp_send.at[it, to[1]], rp_all.at[it, gy], ps.at[it, off], pr.at[it, off], to
        )

    def m_copy(it):
        return remote(p_send.at[it], p_recv.at[it], ms.at[it], mr.at[it], mate)

    root_copy = remote(root_h, rinv2.at[1], xs, xr, mate)

    for it in range(ITERS):
        if it == 0:
            loaded["start"].wait()
        for j in range(8):
            source = start_v if it == 0 else solb
            local[j * block : (j + 1) * block, :] = source[perm[j]]
        if it == 0:
            loaded["op"].wait()
        right = local[...]
        for pair in PAIRS:
            left = jnp.concatenate([op_v[inverse[f]] for f in pair], axis=0)
            both = dot(left, right)
            for k, f in enumerate(pair):
                prod[it, f] = both[k * block : (k + 1) * block]
            if it:
                send_pair(it, pair)
        if it == 0:
            loaded["modes"].wait()
            loaded["loads"].wait()
            loaded["rw"].wait()
            modes_s[...] = split_rows(modes_v[...])
            pl.semaphore_wait(barrier, len(greeted))
            for pair in PAIRS:
                send_pair(it, pair)
            root_copy.start()
            for off in range(1, ny):
                r_copy(off).start()
            modes_t[...] = deep_left(modes_v[...], modes_t.shape[1])
            g = jnp.dot(rw_v[...], modes_v[...], precision=HIGH, preferred_element_type=F32)
            g_t[...] = deep_left(g, g_t.shape[1])
            loaded["w"].wait()
            for f in range(8):
                wb[f] = jnp.broadcast_to(w_v[f : f + 1, :], (block, block)).T
            for k in range(nchip):
                for i in range(ITERS):
                    z_all[i, 2 * k + 1 - core] = jnp.zeros(z_all.shape[2:], F32)
            g_out = pltpu.make_async_copy(g_t, g_o, out_sem.at[0])
            g_out.start()

        coarse = None
        for pair in (PAIRS[3], PAIRS[2], PAIRS[0], PAIRS[1]):
            for f in pair:
                if f < 6:

                    @pl.when(has[f])
                    def _(it=it, f=f):
                        halo_copy(it, f ^ 1).wait_recv()

                    res[f] = loads_v[f].astype(F32) - (prod[it, f] + halo[it, f])
                else:
                    res[f] = loads_v[f].astype(F32) - prod[it, f]
            f = pair[0]
            part = rows_dot(
                modes_s[:, f * block : (f + 2) * block], res[f : f + 2].reshape(2 * block, -1)
            )
            coarse = part if coarse is None else coarse + part
        c_all[it, gz] = coarse
        t_all[it, gz] = jnp.dot(
            rw_v[...], coarse, precision=HIGH, preferred_element_type=F32
        )
        for off in far_first(nz):
            t_copy(it, off).start()
        for off in far_first(nz):
            c_copy(it, off).start()
        if it == 0:
            for off in range(1, ny):
                r_copy(off).wait_recv()
            loaded["rinv"].wait()
            rblk_s[...] = split_rows(rblk[...].reshape(rblk_s.shape[0] // 3, -1))
            root_copy.wait_recv()
            loaded["root"].wait()
            rinv_s[...] = split_rows(rinv2[...].reshape(rinv_s.shape[0] // 3, -1))
        for off in range(1, nz):
            t_copy(it, off).wait_recv()
        total = t_all[it, 0]
        for b in range(1, nz):
            total = total + t_all[it, b]
        s_all[it, gy] = total
        for off in far_first(ny):
            s_copy(it, off).start()
        for off in range(1, ny):
            s_copy(it, off).wait_recv()
        total = s_all[it, 0]
        for a in range(1, ny):
            total = total + s_all[it, a]
        z_all[it, gx] = total
        for off in far_first(nchip):
            z_copy(it, off).start()
        for off in range(1, nz):
            c_copy(it, off).wait_recv()
        part = rows_dot(rblk_s[...], c_all[it].reshape(width, -1))
        rp_send[it] = part.reshape(rp_send.shape[1:])
        rp_all[it, gy] = rp_send[it, gy]
        for off in far_first(ny):
            rp_copy(it, off).start()
        for f in range(8):
            old = start_v[f].astype(F32) if it == 0 else sol[f]
            scale = wb[f]
            sol[f] = old + jnp.concatenate([scale] * (old.shape[1] // block), axis=1) * res[f]
        for off in range(1, ny):
            rp_copy(it, off).wait_recv()
        region = rp_all[it, 0]
        for a in range(1, ny):
            region = region + rp_all[it, a]
        depth = modes_t.shape[1]
        sol[...] = sol[...] + dot(modes_t[...], deep_right(region, depth)).reshape(sol.shape)
        if it == ITERS - 1:
            base_out = pltpu.make_async_copy(sol, base_o, out_sem.at[1])
            base_out.start()
        for off in range(1, nchip):
            z_copy(it, off).wait_recv()
        stack = z_all[it].reshape(nx * z_all.shape[2], -1)
        both = rows_dot(rinv_s[...], stack)
        rm = both.shape[0] // 2
        p_send[it] = both[rm:]
        m_copy(it).start()
        m_copy(it).wait_recv()
        root = both[:rm] + p_recv[it]
        if it < ITERS - 1:
            depth = g_t.shape[1]
            new = sol[...] + dot(g_t[...], deep_right(root, depth)).reshape(sol.shape)
            sol[...] = new
            solb[...] = new.astype(BF16)
        else:
            root_v[...] = root

    root_out = pltpu.make_async_copy(root_v, root_o, out_sem.at[2])
    root_out.start()
    for it in range(ITERS):
        for f in range(6):

            @pl.when(has[f])
            def _(it=it, f=f):
                halo_copy(it, f).wait_send()

        for off in range(1, nz):
            t_copy(it, off).wait_send()
            c_copy(it, off).wait_send()
        for off in range(1, ny):
            s_copy(it, off).wait_send()
            rp_copy(it, off).wait_send()
        for off in range(1, nchip):
            z_copy(it, off).wait_send()
        m_copy(it).wait_send()
    for off in range(1, ny):
        r_copy(off).wait_send()
    root_copy.wait_send()
    g_out.wait()
    base_out.wait()
    root_out.wait()


def last_update(base, g, root, out):
    out[...] = base[...] + dot(g[...], deep_right(root[...], g.shape[1]))


def per_device(
    nx, ny, nz, loads, start, interface_op, block_order, interface_weights, coarse_modes,
    region_weights, region_inverse, root_inverse,
):
    iface, cases = loads.shape[-2:]
    block = iface // 8
    modes_n, rm = region_weights.shape[-2:]
    nchip = nx // 2
    width = nz * modes_n
    faces = (8, block, cases)
    deep_m, deep_g = pad_to(6 * modes_n, 128), pad_to(6 * rm, 128)
    any_spec = pl.BlockSpec(memory_space=pltpu.HBM)
    dma = pltpu.SemaphoreType.DMA
    base, g, root = pl.pallas_call(
        functools.partial(kernel, nx, ny, nz),
        out_shape=(
            jax.ShapeDtypeStruct(faces, F32),
            jax.ShapeDtypeStruct((iface, deep_g), BF16),
            jax.ShapeDtypeStruct((rm, cases), F32),
        ),
        in_specs=[pl.BlockSpec(memory_space=pltpu.SMEM)] + [any_spec] * 8,
        out_specs=(any_spec,) * 3,
        scratch_shapes=[
            pltpu.VMEM(faces, BF16),
            pltpu.VMEM(faces, BF16),
            pltpu.VMEM((8, block, iface), BF16),
            pltpu.VMEM((8, block), F32),
            pltpu.VMEM((modes_n, iface), F32),
            pltpu.VMEM((rm, modes_n), F32),
            pltpu.VMEM((iface, cases), BF16),
            pltpu.VMEM((ITERS, *faces), F32),
            pltpu.VMEM((ITERS, 6, block, cases), F32),
            pltpu.VMEM(faces, F32),
            pltpu.VMEM(faces, BF16),
            pltpu.VMEM(faces, F32),
            pltpu.VMEM((8, block, block), F32),
            pltpu.VMEM((3 * modes_n, iface), BF16),
            pltpu.VMEM((iface, deep_m), BF16),
            pltpu.VMEM((iface, deep_g), BF16),
            pltpu.VMEM((ny, modes_n, width), F32),
            pltpu.VMEM((3 * ny * modes_n, width), BF16),
            pltpu.VMEM((2, rm, nx * rm), F32),
            pltpu.VMEM((6 * rm, nx * rm), BF16),
            pltpu.VMEM((ITERS, nz, rm, cases), F32),
            pltpu.VMEM((ITERS, nz, modes_n, cases), F32),
            pltpu.VMEM((ITERS, ny, rm, cases), F32),
            pltpu.VMEM((ITERS, ny, modes_n, cases), F32),
            pltpu.VMEM((ITERS, ny, modes_n, cases), F32),
            pltpu.VMEM((ITERS, nx, rm, cases), F32),
            pltpu.VMEM((ITERS, rm, cases), F32),
            pltpu.VMEM((ITERS, rm, cases), F32),
            pltpu.VMEM((rm, cases), F32),
            dma((8,)),
            dma((ITERS, 6)), dma((ITERS, 6)),
            dma((ITERS, nz)), dma((ITERS, nz)),
            dma((ITERS, nz)), dma((ITERS, nz)),
            dma((ITERS, ny)), dma((ITERS, ny)),
            dma((ITERS, nchip)), dma((ITERS, nchip)),
            dma((ny,)), dma((ny,)),
            dma((ITERS, ny)), dma((ITERS, ny)),
            dma((ITERS,)), dma((ITERS,)),
            dma(()), dma(()),
            dma((3,)),
        ],
        compiler_params=pltpu.CompilerParams(
            collective_id=0, has_side_effects=True, vmem_limit_bytes=67043328
        ),
        name="iterate",
    )(
        block_order.reshape(8),
        loads.reshape(faces),
        start.reshape(faces),
        interface_op.reshape(8, block, iface),
        interface_weights.reshape(8, block),
        coarse_modes.reshape(modes_n, iface),
        region_weights.reshape(modes_n, rm).T,
        region_inverse.reshape(modes_n, -1),
        root_inverse,
    )
    steps = 4
    out = pl.pallas_call(
        last_update,
        grid=(steps,),
        out_shape=jax.ShapeDtypeStruct((iface, cases), F32),
        in_specs=[
            pl.BlockSpec((iface // steps, cases), lambda i: (i, 0)),
            pl.BlockSpec((iface // steps, deep_g), lambda i: (i, 0)),
            pl.BlockSpec((rm, cases), lambda i: (0, 0)),
        ],
        out_specs=pl.BlockSpec((iface // steps, cases), lambda i: (i, 0)),
        name="last_update",
    )(base.reshape(iface, cases), g, root)
    return out.reshape(1, 1, 1, iface, cases)


def solution(mesh):
    nx, ny, nz = (mesh.shape[axis] for axis in ("gx", "gy", "gz"))
    placed = (
        P("gx", "gy", "gz", None, None),
        P("gx", "gy", "gz", None, None),
        P("gx", "gy", "gz", None, None),
        P("gx", "gy", "gz", None),
        P("gx", "gy", "gz", None),
        P("gx", "gy", "gz", None, None),
        P("gx", "gy", "gz", None, None),
        P("gx", ("gy", "gz"), None),
        P("gx", None),
    )
    return jax.shard_map(
        functools.partial(per_device, nx, ny, nz),
        mesh=mesh,
        in_specs=placed,
        out_specs=P("gx", "gy", "gz", None, None),
        check_vma=False,
    )
```

time: 254 us -> 76 us (0.30); the launches traced: 251 us -> 75.8 us
  blocking collectives: 89.1 us -> 0 us
  Pallas kernels: 0 us -> 75.8 us
  starting transfers between devices: 55.9 us -> 0 us
  waiting for transfers between devices: 43.1 us -> 0 us
  local copies, waits for them, and re-layouts: 30.2 us -> 0 us
  matrix products: 24.9 us -> 0 us
  other arithmetic: 7.53 us -> 0 us
    all_to_all x2 -> x0, blocking collectives: 89.1 us -> none  [sent_to_all(): return lax.all_to_all(copies, axis, split_axis=0, concat_axis=0, tiled=True)]
    pallas_call x0 -> x2, Pallas kernels: none -> 75.8 us  [the longest x1 72.1 us: per_device(): pl.pallas_call(functools.partial(kernel, nx, ny, nz), out_shape=(jax.Shap...]
    all_to_all x2 -> x0, starting transfers between devices: 30.5 us -> none  [sent_to_all(): return lax.all_to_all(copies, axis, split_axis=0, concat_axis=0, tiled=True)]
    all_to_all x2 -> x0, waiting for transfers between devices: 25.7 us -> none  [sent_to_all(): return lax.all_to_all(copies, axis, split_axis=0, concat_axis=0, tiled=True)]
    ppermute x12 -> x0, starting transfers between devices: 25.3 us -> none  [the longest x6 15.9 us: with_halo(): lax.ppermute(tail, axis, [(i, (i + 1) % count) for i in range(ends)])]
    dot_general x14 -> x0, matrix products: 24.9 us -> none  [the longest x4 9.03 us: transpose_dot(): lax.dot_general(left, right, (((0,), (0,)), ((), ())), precision=HIGH, pr...]
    ppermute x12 -> x0, waiting for transfers between devices: 17.4 us -> none  [the longest x6 11 us: with_halo(): lax.ppermute(tail, axis, [(i, (i + 1) % count) for i in range(ends)])]
    reshape x6 -> x0, local copies, waits for them, and re-layouts: 9.05 us -> none  [the longest x2 2.65 us: per_device(): assembled = jnp.concatenate([(product[0] + padded_x[0])[None], (product[1...]
  transfers between devices with their start and end apart: 14 -> 0, of which waited for: 9 -> 0; matrix products, arithmetic and copies ran while one was open for 8% -> 0% of each run, Pallas kernels for 0% -> 0%
where the time goes in v1:
time: 76 us; the launch traced here: 75.8 us
  Pallas kernels  75.8 us (100%)
    pallas_call x1, Pallas kernels, per_device(): pl.pallas_call(functools.partial(kernel, nx, ny, nz), out_shape=(jax.Shap...  72.1 us
    pallas_call x1, Pallas kernels, per_device(): pl.pallas_call(last_update, grid=(steps,), out_shape=jax.ShapeDtypeStruct...  3.69 us

profile of v1, /device:TPU:1, one launch (start us, length us, event | category | flops | bytes accessed | tf_op | source)
XLA Modules:
  0.0 75.8 jit_solution(7143032881659944780)
XLA Ops:
  0.0 72.1 %iterate.1 = (f32[8,128,256]{2,1,0:T(8,128)}, bf16[1024,128]{1,0:T(8,128)(2,1)}, f32[16,256]{1,0:T(8,128)}) custom-call(s32[8]{0:T(128)} %bitcast.20, bf16[8,128,256]{2,1,0:T(8,128)(2,1)} %bitcast.14, bf16[8,128,256]{2,1,0:T(8,128)(2,1)} %bitcast.15, bf16[8,128,1024]{2,1,0:T(8,128)(2,1)} %bitcast.12, f32[8,128]{1,0:T(8,128)} %bitcast.19, ...), custom_call_target="tpu_custom_call" | custom-call | tf_op jit(solution)/shard_map/iterate/pallas_call | solution.py:360
  72.1 3.7 %last_update.1 = f32[1024,256]{1,0:T(8,128)} custom-call(f32[1024,256]{1,0:T(8,128)} %bitcast.13, bf16[1024,128]{1,0:T(8,128)(2,1)} %get-tuple-element.9.g, f32[16,256]{1,0:T(8,128)} %get-tuple-element.10.root), custom_call_target="tpu_custom_call" | custom-call | tf_op jit(solution)/shard_map/last_update/pallas_call | solution.py:427

commit v2 on v1

--- a/solution.py
+++ b/solution.py
@@ -67,25 +67,28 @@
     perm_s, loads_h, start_h, op_h, w_h, modes_h, rw_h, rinv_h, root_h,
     base_o, g_o, root_o,
     loads_v, start_v, op_v, w_v, modes_v, rw_v,
-    local, prod, halo, sol, solb, res, wb, modes_s, modes_t, g_t,
+    local, prod, halo, sol, solb, wb, pair_s, modes_t, g_t, nbm,
     rblk, rblk_s, rinv2, rinv_s,
-    t_all, c_all, s_all, rp_send, rp_all, z_all, p_send, p_recv, root_v,
-    in_sem, hs, hr, ts, tr, cs, cr, ss, sr, zs, zr, rs, rr, ps, pr, ms, mr, xs, xr, out_sem,
+    kb_send, kb, t_send, tx, ty, c_all, rp_send, rp_all, z_all, f_send, f_all, root_v,
+    in_sem, hs, hr, ns, nr, ks, kr, ts, tr, ys, yr, cs, cr, zs, zr, rs, rr, ps, pr, fs, fr, xs, xr,
+    out_sem,
 ):
     gx, gy, gz = lax.axis_index("gx"), lax.axis_index("gy"), lax.axis_index("gz")
     nchip = nx // 2
     chip, core = gx // 2, lax.rem(gx, 2)
+    half = gy // 2
     modes_n, iface = modes_v.shape
     block = iface // 8
     width = nz * modes_n
-    mate = (gx + 1 - 2 * core, gy, gz)
+    mate_x = gx + 1 - 2 * core
+    mate = (mate_x, gy, gz)
     beside = (lax.rem(gx + 2 * core - 1 + nx, nx), gy, gz)
 
     def along_z(off):
         return (gx, gy, lax.rem(gz + off, nz))
 
-    def along_y(off):
-        return (gx, lax.rem(gy + off, ny), gz)
+    def along_y(off, x=gx):
+        return (x, lax.rem(gy + off, ny), gz)
 
     def along_x(off):
         return (lax.rem(chip + off, nchip) * 2 + core, gy, gz)
@@ -114,7 +117,8 @@
     barrier = pltpu.get_barrier_semaphore()
     greeted = (
         [along_x(o) for o in far_first(nchip)] + [along_z(o) for o in far_first(nz)]
-        + [along_y(o) for o in far_first(ny)] + [beside, mate]
+        + [along_y(o) for o in far_first(ny)] + [along_y(o, mate_x) for o in far_first(ny)]
+        + [beside, mate]
     )
     for device in greeted:
         pl.semaphore_signal(barrier, inc=1, device_id=device, device_id_type=MESH)
@@ -130,12 +134,60 @@
             prod.at[it, f], halo.at[it, f ^ 1], hs.at[it, f], hr.at[it, f ^ 1], towards[f]
         )
 
-    for it in range(ITERS):
-        for f in range(6):
-
-            @pl.when(jnp.logical_not(has[f]))
-            def _(it=it, f=f):
+    def modes_copy(f):
+        face = modes_h.at[:, f * block : (f + 1) * block]
+        return remote(face, nbm.at[f ^ 1], ns.at[f], nr.at[f ^ 1], towards[f])
+
+    def kb_copy(it, f):
+        return remote(
+            kb_send.at[it, f], kb.at[it, f ^ 1], ks.at[it, f], kr.at[it, f ^ 1], towards[f]
+        )
+
+    def t_copy(it, off):
+        to = along_y(off)
+        return remote(t_send.at[it, to[1]], tx.at[it, gy], ts.at[it, off], tr.at[it, off], to)
+
+    def y_copy(it, off):
+        return remote(ty.at[it, gz], ty.at[it, gz], ys.at[it, off], yr.at[it, off], along_z(off))
+
+    def c_copy(it, off):
+        return remote(
+            c_all.at[it, gz], c_all.at[it, gz], cs.at[it, off], cr.at[it, off], along_z(off)
+        )
+
+    def z_rows(h):
+        return pl.ds(pl.multiple_of(h * 8, 8), 8)
+
+    def z_copy(it, off):
+        tile = z_all.at[it, gx, z_rows(half)]
+        return remote(tile, tile, zs.at[it, off], zr.at[it, off], along_x(off))
+
+    def r_copy(off):
+        to = along_y(off)
+        return remote(rinv_h.at[:, columns(to[1])], rblk.at[gy], rs.at[off], rr.at[off], to)
+
+    def rp_copy(it, off):
+        to = along_y(off)
+        return remote(
+            rp_send.at[it, to[1]], rp_all.at[it, gy], ps.at[it, off], pr.at[it, off], to
+        )
+
+    def f_copy(it, other, off):
+        at = (it, other, off)
+        to = along_y(off, mate_x if other else gx)
+        return remote(f_send.at[it, other], f_all.at[it, core, gy], fs.at[at], fr.at[at], to)
+
+    root_copy = remote(root_h, rinv2.at[1], xs, xr, mate)
+    finals = [(1, o) for o in (2, 1, 3, 0) if o < ny] + [(0, o) for o in far_first(ny)]
+
+    for f in range(6):
+
+        @pl.when(jnp.logical_not(has[f]))
+        def _(f=f):
+            nbm[f] = jnp.zeros_like(nbm[f])
+            for it in range(ITERS):
                 halo[it, f] = jnp.zeros_like(halo[it, f])
+                kb[it, f] = jnp.zeros_like(kb[it, f])
 
     perm = [perm_s[j] for j in range(8)]
     inverse = []
@@ -145,113 +197,116 @@
             at = jnp.where(perm[j] == f, j, at)
         inverse.append(at)
 
-    def send_pair(it, pair):
-        for f in pair:
+    def on_faces(faces, action):
+        for f in faces:
             if f < 6:
 
                 @pl.when(has[f])
-                def _(it=it, f=f):
-                    halo_copy(it, f).start()
-
-    def t_copy(it, off):
-        return remote(
-            t_all.at[it, gz], t_all.at[it, gz], ts.at[it, off], tr.at[it, off], along_z(off)
-        )
-
-    def c_copy(it, off):
-        return remote(
-            c_all.at[it, gz], c_all.at[it, gz], cs.at[it, off], cr.at[it, off], along_z(off)
-        )
-
-    def s_copy(it, off):
-        return remote(
-            s_all.at[it, gy], s_all.at[it, gy], ss.at[it, off], sr.at[it, off], along_y(off)
-        )
-
-    def z_copy(it, off):
-        return remote(
-            z_all.at[it, gx], z_all.at[it, gx], zs.at[it, off], zr.at[it, off], along_x(off)
-        )
-
-    def r_copy(off):
-        to = along_y(off)
-        return remote(rinv_h.at[:, columns(to[1])], rblk.at[gy], rs.at[off], rr.at[off], to)
-
-    def rp_copy(it, off):
-        to = along_y(off)
-        return remote(
-            rp_send.at[it, to[1]], rp_all.at[it, gy], ps.at[it, off], pr.at[it, off], to
-        )
-
-    def m_copy(it):
-        return remote(p_send.at[it], p_recv.at[it], ms.at[it], mr.at[it], mate)
-
-    root_copy = remote(root_h, rinv2.at[1], xs, xr, mate)
-
+                def _(f=f):
+                    action(f)
+
+    loads_c = None
     for it in range(ITERS):
+
+        def products(it, pair):
+            left = jnp.concatenate([op_v[inverse[f]] for f in pair], axis=0)
+            both = dot(left, local[...])
+            for k, f in enumerate(pair):
+                prod[it, f] = both[k * block : (k + 1) * block]
+
+        def contributions(it, p):
+            pair = PAIRS[p]
+            rows = 3 * modes_n * (3 if pair[0] < 6 else 1)
+            got = rows_dot(
+                pair_s[p, :rows], prod[it, pair[0] : pair[0] + 2].reshape(2 * block, -1)
+            )
+            if pair[0] < 6:
+                kb_send[it, pair[0]] = got[modes_n : 2 * modes_n]
+                kb_send[it, pair[1]] = got[2 * modes_n :]
+                on_faces(pair, lambda f: kb_copy(it, f).start())
+            return got[:modes_n]
+
         if it == 0:
             loaded["start"].wait()
         for j in range(8):
             source = start_v if it == 0 else solb
             local[j * block : (j + 1) * block, :] = source[perm[j]]
+        own = []
         if it == 0:
             loaded["op"].wait()
-        right = local[...]
-        for pair in PAIRS:
-            left = jnp.concatenate([op_v[inverse[f]] for f in pair], axis=0)
-            both = dot(left, right)
-            for k, f in enumerate(pair):
-                prod[it, f] = both[k * block : (k + 1) * block]
-            if it:
-                send_pair(it, pair)
-        if it == 0:
+            for pair in PAIRS:
+                products(it, pair)
             loaded["modes"].wait()
             loaded["loads"].wait()
             loaded["rw"].wait()
-            modes_s[...] = split_rows(modes_v[...])
             pl.semaphore_wait(barrier, len(greeted))
-            for pair in PAIRS:
-                send_pair(it, pair)
-            root_copy.start()
-            for off in range(1, ny):
-                r_copy(off).start()
+            on_faces(range(6), lambda f: modes_copy(f).start())
+            modes_rows = split_rows(modes_v[...])
+            loads_c = None
+            for f in range(8):
+                got = dot(modes_rows[:, f * block : (f + 1) * block], loads_v[f])
+                loads_c = got if loads_c is None else loads_c + got
+            n = modes_n
+            loads_c = (loads_c[2 * n :] + loads_c[n : 2 * n]) + loads_c[:n]
             modes_t[...] = deep_left(modes_v[...], modes_t.shape[1])
             g = jnp.dot(rw_v[...], modes_v[...], precision=HIGH, preferred_element_type=F32)
             g_t[...] = deep_left(g, g_t.shape[1])
             loaded["w"].wait()
             for f in range(8):
                 wb[f] = jnp.broadcast_to(w_v[f : f + 1, :], (block, block)).T
-            for k in range(nchip):
-                for i in range(ITERS):
+            pair_s[3, : 3 * n] = modes_rows[:, 6 * block :]
+            for p in range(3):
+                pair = PAIRS[p]
+                on_faces(pair, lambda f: modes_copy(f ^ 1).wait_recv())
+                fill = jnp.zeros((n, block), F32)
+                pair_s[p] = split_rows(
+                    jnp.concatenate([
+                        modes_v[:, pair[0] * block : (pair[0] + 2) * block],
+                        jnp.concatenate([nbm[pair[0]], fill], axis=1),
+                        jnp.concatenate([fill, nbm[pair[1]]], axis=1),
+                    ], axis=0)
+                )
+                own.append(contributions(it, p))
+            own.append(contributions(it, 3))
+        else:
+            for p, pair in enumerate(PAIRS):
+                products(it, pair)
+                own.append(contributions(it, p))
+        on_faces((2, 3, 0, 1), lambda f: halo_copy(it, f).start())
+        if it == 0:
+            root_copy.start()
+            for off in range(1, ny):
+                r_copy(off).start()
+            for i in range(ITERS):
+                for k in range(nchip):
                     z_all[i, 2 * k + 1 - core] = jnp.zeros(z_all.shape[2:], F32)
+                    z_all[i, 2 * k + core, z_rows(1 - half)] = jnp.zeros((8, z_all.shape[3]), F32)
             g_out = pltpu.make_async_copy(g_t, g_o, out_sem.at[0])
             g_out.start()
 
-        coarse = None
-        for pair in (PAIRS[3], PAIRS[2], PAIRS[0], PAIRS[1]):
-            for f in pair:
-                if f < 6:
-
-                    @pl.when(has[f])
-                    def _(it=it, f=f):
-                        halo_copy(it, f ^ 1).wait_recv()
-
-                    res[f] = loads_v[f].astype(F32) - (prod[it, f] + halo[it, f])
-                else:
-                    res[f] = loads_v[f].astype(F32) - prod[it, f]
-            f = pair[0]
-            part = rows_dot(
-                modes_s[:, f * block : (f + 2) * block], res[f : f + 2].reshape(2 * block, -1)
-            )
-            coarse = part if coarse is None else coarse + part
+        coarse = loads_c - (own[0] + own[1] + own[2] + own[3])
+        for f in (0, 1, 2, 3, 4, 5):
+            on_faces((f,), lambda f: kb_copy(it, f ^ 1).wait_recv())
+            coarse = coarse - kb[it, f]
         c_all[it, gz] = coarse
-        t_all[it, gz] = jnp.dot(
-            rw_v[...], coarse, precision=HIGH, preferred_element_type=F32
-        )
+        t = jnp.dot(rw_v[...], coarse, precision=HIGH, preferred_element_type=F32)
+        lanes = t.shape[1] // 2
+        for q in range(4):
+            t_send[it, q] = t[8 * (q // 2) : 8 * (q // 2) + 8, lanes * (q % 2) : lanes * (q % 2 + 1)]
+        for off in far_first(ny):
+            t_copy(it, off).start()
+        tx[it, gy] = t_send[it, gy]
+        for off in range(1, ny):
+            t_copy(it, off).wait_recv()
+        total = tx[it, 0]
+        for a in range(1, ny):
+            total = total + tx[it, a]
+        ty[it, gz] = total
         for off in far_first(nz):
-            t_copy(it, off).start()
+            y_copy(it, off).start()
         for off in far_first(nz):
             c_copy(it, off).start()
+        on_faces((4, 5), lambda f: halo_copy(it, f).start())
         if it == 0:
             for off in range(1, ny):
                 r_copy(off).wait_recv()
@@ -261,19 +316,11 @@
             loaded["root"].wait()
             rinv_s[...] = split_rows(rinv2[...].reshape(rinv_s.shape[0] // 3, -1))
         for off in range(1, nz):
-            t_copy(it, off).wait_recv()
-        total = t_all[it, 0]
+            y_copy(it, off).wait_recv()
+        total = ty[it, 0]
         for b in range(1, nz):
-            total = total + t_all[it, b]
-        s_all[it, gy] = total
-        for off in far_first(ny):
-            s_copy(it, off).start()
-        for off in range(1, ny):
-            s_copy(it, off).wait_recv()
-        total = s_all[it, 0]
-        for a in range(1, ny):
-            total = total + s_all[it, a]
-        z_all[it, gx] = total
+            total = total + ty[it, b]
+        z_all[it, gx, z_rows(half)] = total
         for off in far_first(nchip):
             z_copy(it, off).start()
         for off in range(1, nz):
@@ -283,10 +330,12 @@
         rp_all[it, gy] = rp_send[it, gy]
         for off in far_first(ny):
             rp_copy(it, off).start()
-        for f in range(8):
+        for f in (6, 7, 0, 1, 2, 3, 4, 5):
+            on_faces((f,), lambda f: halo_copy(it, f ^ 1).wait_recv())
+            whole = prod[it, f] + halo[it, f] if f < 6 else prod[it, f]
             old = start_v[f].astype(F32) if it == 0 else sol[f]
-            scale = wb[f]
-            sol[f] = old + jnp.concatenate([scale] * (old.shape[1] // block), axis=1) * res[f]
+            scale = jnp.concatenate([wb[f]] * (old.shape[1] // block), axis=1)
+            sol[f] = old + scale * (loads_v[f].astype(F32) - whole)
         for off in range(1, ny):
             rp_copy(it, off).wait_recv()
         region = rp_all[it, 0]
@@ -302,10 +351,17 @@
         stack = z_all[it].reshape(nx * z_all.shape[2], -1)
         both = rows_dot(rinv_s[...], stack)
         rm = both.shape[0] // 2
-        p_send[it] = both[rm:]
-        m_copy(it).start()
-        m_copy(it).wait_recv()
-        root = both[:rm] + p_recv[it]
+        f_send[it, 0] = both[:rm]
+        f_send[it, 1] = both[rm:]
+        for other, off in finals:
+            f_copy(it, other, off).start()
+        f_all[it, core, gy] = both[:rm]
+        for other, off in finals:
+            f_copy(it, other, off).wait_recv()
+        root = jnp.concatenate([
+            (f_all[it, 0, k] + f_all[it, 1, k]) + (f_all[it, 0, 2 + k] + f_all[it, 1, 2 + k])
+            for k in range(2)
+        ], axis=1)
         if it < ITERS - 1:
             depth = g_t.shape[1]
             new = sol[...] + dot(g_t[...], deep_right(root, depth)).reshape(sol.shape)
@@ -316,22 +372,20 @@
 
     root_out = pltpu.make_async_copy(root_v, root_o, out_sem.at[2])
     root_out.start()
+    on_faces(range(6), lambda f: modes_copy(f).wait_send())
     for it in range(ITERS):
-        for f in range(6):
-
-            @pl.when(has[f])
-            def _(it=it, f=f):
-                halo_copy(it, f).wait_send()
-
+        on_faces(range(6), lambda f: halo_copy(it, f).wait_send())
+        on_faces(range(6), lambda f: kb_copy(it, f).wait_send())
         for off in range(1, nz):
-            t_copy(it, off).wait_send()
+            y_copy(it, off).wait_send()
             c_copy(it, off).wait_send()
         for off in range(1, ny):
-            s_copy(it, off).wait_send()
+            t_copy(it, off).wait_send()
             rp_copy(it, off).wait_send()
         for off in range(1, nchip):
             z_copy(it, off).wait_send()
-        m_copy(it).wait_send()
+        for other, off in finals:
+            f_copy(it, other, off).wait_send()
     for off in range(1, ny):
         r_copy(off).wait_send()
     root_copy.wait_send()
@@ -340,8 +394,25 @@
     root_out.wait()
 
 
-def last_update(base, g, root, out):
-    out[...] = base[...] + dot(g[...], deep_right(root[...], g.shape[1]))
+def last_update(base_h, g_h, root_h, out_h, base, g, root, out, sem, out_sem):
+    steps = base.shape[0]
+    copies = [
+        pltpu.make_async_copy(root_h, root, sem.at[0]),
+        pltpu.make_async_copy(g_h, g, sem.at[1]),
+    ] + [pltpu.make_async_copy(base_h.at[i], base.at[i], sem.at[2 + i]) for i in range(steps)]
+    for copy in copies:
+        copy.start()
+    copies[0].wait()
+    copies[1].wait()
+    right = deep_right(root[...], g.shape[-1])
+    sent = []
+    for i in range(steps):
+        copies[2 + i].wait()
+        out[i] = base[i] + dot(g[i], right)
+        sent.append(pltpu.make_async_copy(out.at[i], out_h.at[i], out_sem.at[i]))
+        sent[-1].start()
+    for copy in sent:
+        copy.wait()
 
 
 def per_device(
@@ -378,33 +449,38 @@
             pltpu.VMEM((ITERS, 6, block, cases), F32),
             pltpu.VMEM(faces, F32),
             pltpu.VMEM(faces, BF16),
-            pltpu.VMEM(faces, F32),
             pltpu.VMEM((8, block, block), F32),
-            pltpu.VMEM((3 * modes_n, iface), BF16),
+            pltpu.VMEM((4, 9 * modes_n, 2 * block), BF16),
             pltpu.VMEM((iface, deep_m), BF16),
             pltpu.VMEM((iface, deep_g), BF16),
+            pltpu.VMEM((6, modes_n, block), F32),
             pltpu.VMEM((ny, modes_n, width), F32),
             pltpu.VMEM((3 * ny * modes_n, width), BF16),
             pltpu.VMEM((2, rm, nx * rm), F32),
             pltpu.VMEM((6 * rm, nx * rm), BF16),
-            pltpu.VMEM((ITERS, nz, rm, cases), F32),
+            pltpu.VMEM((ITERS, 6, modes_n, cases), F32),
+            pltpu.VMEM((ITERS, 6, modes_n, cases), F32),
+            pltpu.VMEM((ITERS, 4, rm // 2, cases // 2), F32),
+            pltpu.VMEM((ITERS, ny, rm // 2, cases // 2), F32),
+            pltpu.VMEM((ITERS, nz, rm // 2, cases // 2), F32),
             pltpu.VMEM((ITERS, nz, modes_n, cases), F32),
-            pltpu.VMEM((ITERS, ny, rm, cases), F32),
             pltpu.VMEM((ITERS, ny, modes_n, cases), F32),
             pltpu.VMEM((ITERS, ny, modes_n, cases), F32),
-            pltpu.VMEM((ITERS, nx, rm, cases), F32),
-            pltpu.VMEM((ITERS, rm, cases), F32),
-            pltpu.VMEM((ITERS, rm, cases), F32),
+            pltpu.VMEM((ITERS, nx, rm, cases // 2), F32),
+            pltpu.VMEM((ITERS, 2, rm, cases // 2), F32),
+            pltpu.VMEM((ITERS, 2, ny, rm, cases // 2), F32),
             pltpu.VMEM((rm, cases), F32),
             dma((8,)),
             dma((ITERS, 6)), dma((ITERS, 6)),
+            dma((6,)), dma((6,)),
+            dma((ITERS, 6)), dma((ITERS, 6)),
+            dma((ITERS, ny)), dma((ITERS, ny)),
             dma((ITERS, nz)), dma((ITERS, nz)),
             dma((ITERS, nz)), dma((ITERS, nz)),
-            dma((ITERS, ny)), dma((ITERS, ny)),
             dma((ITERS, nchip)), dma((ITERS, nchip)),
             dma((ny,)), dma((ny,)),
             dma((ITERS, ny)), dma((ITERS, ny)),
-            dma((ITERS,)), dma((ITERS,)),
+            dma((ITERS, 2, ny)), dma((ITERS, 2, ny)),
             dma(()), dma(()),
             dma((3,)),
         ],
@@ -424,18 +500,23 @@
         root_inverse,
     )
     steps = 4
+    rows = (steps, iface // steps)
     out = pl.pallas_call(
         last_update,
-        grid=(steps,),
-        out_shape=jax.ShapeDtypeStruct((iface, cases), F32),
-        in_specs=[
-            pl.BlockSpec((iface // steps, cases), lambda i: (i, 0)),
-            pl.BlockSpec((iface // steps, deep_g), lambda i: (i, 0)),
-            pl.BlockSpec((rm, cases), lambda i: (0, 0)),
+        out_shape=jax.ShapeDtypeStruct((*rows, cases), F32),
+        in_specs=[any_spec] * 3,
+        out_specs=any_spec,
+        scratch_shapes=[
+            pltpu.VMEM((*rows, cases), F32),
+            pltpu.VMEM((*rows, deep_g), BF16),
+            pltpu.VMEM((rm, cases), F32),
+            pltpu.VMEM((*rows, cases), F32),
+            dma((2 + steps,)),
+            dma((steps,)),
         ],
-        out_specs=pl.BlockSpec((iface // steps, cases), lambda i: (i, 0)),
+        compiler_params=pltpu.CompilerParams(vmem_limit_bytes=67043328),
         name="last_update",
-    )(base.reshape(iface, cases), g, root)
+    )(base.reshape(*rows, cases), g.reshape(*rows, deep_g), root)
     return out.reshape(1, 1, 1, iface, cases)
 
 

time: 76 us -> 78.5 us (1.033)
  Pallas kernels: 75.8 us -> 78.3 us
    pallas_call x1, Pallas kernels: 72.1 us -> 75.7 us  [per_device(): pl.pallas_call(functools.partial(kernel, nx, ny, nz), out_shape=(jax.Shap...]
    pallas_call x1, Pallas kernels: 3.69 us -> 2.61 us  [per_device(): pl.pallas_call(last_update, out_shape=jax.ShapeDtypeStruct((*rows, cases)...]
where the time goes in v2:
time: 78.5 us; the launch traced here: 78.3 us
  Pallas kernels  78.3 us (100%)
    pallas_call x1, Pallas kernels, per_device(): pl.pallas_call(functools.partial(kernel, nx, ny, nz), out_shape=(jax.Shap...  75.7 us
    pallas_call x1, Pallas kernels, per_device(): pl.pallas_call(last_update, out_shape=jax.ShapeDtypeStruct((*rows, cases)...  2.61 us

profile of v2, /device:TPU:1, one launch (start us, length us, event | category | flops | bytes accessed | tf_op | source)
XLA Modules:
  0.0 78.3 jit_solution(2456595102686482690)
XLA Ops:
  0.0 75.7 %iterate.1 = (f32[8,128,256]{2,1,0:T(8,128)}, bf16[1024,128]{1,0:T(8,128)(2,1)}, f32[16,256]{1,0:T(8,128)}) custom-call(s32[8]{0:T(128)} %bitcast.22, bf16[8,128,256]{2,1,0:T(8,128)(2,1)} %bitcast.15, bf16[8,128,256]{2,1,0:T(8,128)(2,1)} %bitcast.16, bf16[8,128,1024]{2,1,0:T(8,128)(2,1)} %bitcast.13, f32[8,128]{1,0:T(8,128)} %bitcast.21, ...), custom_call_target="tpu_custom_call" | custom-call | tf_op jit(solution)/shard_map/iterate/pallas_call | solution.py:431
  75.7 2.6 %last_update.1 = f32[4,256,256]{2,1,0:T(8,128)} custom-call(f32[4,256,256]{2,1,0:T(8,128)} %bitcast.14, bf16[4,256,128]{2,1,0:T(8,128)(2,1)} %bitcast.17, f32[16,256]{1,0:T(8,128)} %get-tuple-element.10.root_h), custom_call_target="tpu_custom_call" | custom-call | tf_op jit(solution)/shard_map/last_update/pallas_call | solution.py:504

commit v3 on v1

--- a/solution.py
+++ b/solution.py
@@ -13,6 +13,7 @@
 BF16 = jnp.bfloat16
 HIGH = lax.Precision.HIGHEST
 PAIRS = ((2, 3), (4, 5), (0, 1), (6, 7))
+FACES = tuple(f for pair in PAIRS for f in pair)
 
 
 def dot(a, b):
@@ -64,13 +65,13 @@
 
 def kernel(
     nx, ny, nz,
-    perm_s, loads_h, start_h, op_h, w_h, modes_h, rw_h, rinv_h, root_h,
+    perm_h, loads_h, start_h, op_h, w_h, modes_h, rw_h, rinv_h, root_h,
     base_o, g_o, root_o,
-    loads_v, start_v, op_v, w_v, modes_v, rw_v,
-    local, prod, halo, sol, solb, res, wb, modes_s, modes_t, g_t,
-    rblk, rblk_s, rinv2, rinv_s,
-    t_all, c_all, s_all, rp_send, rp_all, z_all, p_send, p_recv, root_v,
-    in_sem, hs, hr, ts, tr, cs, cr, ss, sr, zs, zr, rs, rr, ps, pr, ms, mr, xs, xr, out_sem,
+    perm_s, loads_v, start_v, op_v, op_f, w_v, modes_v, rw_v,
+    local, prod, halo, sol, solb, res, wb, modes_s, pair_s, modes_t, g_t, nbm,
+    rblk, rblk_s, rinv2, rinv_s, kb_send, kb,
+    t_all, c_all, s_all, rp_send, rp_all, z_all, p_send, p_recv,
+    in_sem, hs, hr, ns, nr, ks, kr, ts, tr, cs, cr, ss, sr, zs, zr, rs, rr, ps, pr, ms, mr, xs, xr,
 ):
     gx, gy, gz = lax.axis_index("gx"), lax.axis_index("gy"), lax.axis_index("gz")
     nchip = nx // 2
@@ -104,7 +105,7 @@
 
     loaded = {}
     for i, (name, src, dst) in enumerate((
-        ("start", start_h, start_v), ("op", op_h, op_v), ("modes", modes_h, modes_v), ("rw", rw_h, rw_v),
+        ("perm", perm_h, perm_s), ("start", start_h, start_v), ("op", op_h, op_v), ("modes", modes_h, modes_v), ("rw", rw_h, rw_v),
         ("loads", loads_h, loads_v), ("w", w_h, w_v), ("root", root_h, rinv2.at[0]),
         ("rinv", rinv_h.at[:, columns(gy)], rblk.at[gy]),
     )):
@@ -130,13 +131,16 @@
             prod.at[it, f], halo.at[it, f ^ 1], hs.at[it, f], hr.at[it, f ^ 1], towards[f]
         )
 
-    for it in range(ITERS):
-        for f in range(6):
-
-            @pl.when(jnp.logical_not(has[f]))
-            def _(it=it, f=f):
+    for f in range(6):
+
+        @pl.when(jnp.logical_not(has[f]))
+        def _(f=f):
+            nbm[f] = jnp.zeros_like(nbm[f])
+            kb[f] = jnp.zeros_like(kb[f])
+            for it in range(ITERS):
                 halo[it, f] = jnp.zeros_like(halo[it, f])
 
+    loaded["perm"].wait()
     perm = [perm_s[j] for j in range(8)]
     inverse = []
     for f in range(8):
@@ -145,13 +149,20 @@
             at = jnp.where(perm[j] == f, j, at)
         inverse.append(at)
 
-    def send_pair(it, pair):
-        for f in pair:
+    def on_faces(faces, action):
+        for f in faces:
             if f < 6:
 
                 @pl.when(has[f])
-                def _(it=it, f=f):
-                    halo_copy(it, f).start()
+                def _(f=f):
+                    action(f)
+
+    def modes_copy(f):
+        face = modes_h.at[:, f * block : (f + 1) * block]
+        return remote(face, nbm.at[f ^ 1], ns.at[f], nr.at[f ^ 1], towards[f])
+
+    def kb_copy(f):
+        return remote(kb_send.at[f], kb.at[f ^ 1], ks.at[f], kr.at[f ^ 1], towards[f])
 
     def t_copy(it, off):
         return remote(
@@ -188,33 +199,27 @@
 
     root_copy = remote(root_h, rinv2.at[1], xs, xr, mate)
 
+    n = modes_n
+    loads_c = None
     for it in range(ITERS):
         if it == 0:
             loaded["start"].wait()
-        for j in range(8):
-            source = start_v if it == 0 else solb
-            local[j * block : (j + 1) * block, :] = source[perm[j]]
-        if it == 0:
+            for j in range(8):
+                local[j * block : (j + 1) * block, :] = start_v[perm[j]]
             loaded["op"].wait()
-        right = local[...]
-        for pair in PAIRS:
-            left = jnp.concatenate([op_v[inverse[f]] for f in pair], axis=0)
-            both = dot(left, right)
-            for k, f in enumerate(pair):
-                prod[it, f] = both[k * block : (k + 1) * block]
-            if it:
-                send_pair(it, pair)
-        if it == 0:
+            right = local[...]
+            for f in FACES:
+                prod[it, f] = dot(op_v[inverse[f]], right)
+            pl.semaphore_wait(barrier, len(greeted))
+            on_faces(FACES, lambda f: halo_copy(it, f).start())
+            on_faces(range(6), lambda f: modes_copy(f).start())
+            root_copy.start()
+            for off in range(1, ny):
+                r_copy(off).start()
             loaded["modes"].wait()
             loaded["loads"].wait()
             loaded["rw"].wait()
             modes_s[...] = split_rows(modes_v[...])
-            pl.semaphore_wait(barrier, len(greeted))
-            for pair in PAIRS:
-                send_pair(it, pair)
-            root_copy.start()
-            for off in range(1, ny):
-                r_copy(off).start()
             modes_t[...] = deep_left(modes_v[...], modes_t.shape[1])
             g = jnp.dot(rw_v[...], modes_v[...], precision=HIGH, preferred_element_type=F32)
             g_t[...] = deep_left(g, g_t.shape[1])
@@ -224,35 +229,52 @@
             for k in range(nchip):
                 for i in range(ITERS):
                     z_all[i, 2 * k + 1 - core] = jnp.zeros(z_all.shape[2:], F32)
-            g_out = pltpu.make_async_copy(g_t, g_o, out_sem.at[0])
-            g_out.start()
-
-        coarse = None
-        for pair in (PAIRS[3], PAIRS[2], PAIRS[0], PAIRS[1]):
-            for f in pair:
-                if f < 6:
-
-                    @pl.when(has[f])
-                    def _(it=it, f=f):
-                        halo_copy(it, f ^ 1).wait_recv()
-
-                    res[f] = loads_v[f].astype(F32) - (prod[it, f] + halo[it, f])
-                else:
-                    res[f] = loads_v[f].astype(F32) - prod[it, f]
-            f = pair[0]
-            part = rows_dot(
-                modes_s[:, f * block : (f + 2) * block], res[f : f + 2].reshape(2 * block, -1)
-            )
-            coarse = part if coarse is None else coarse + part
+            coarse = None
+            for pair in (PAIRS[3], PAIRS[2], PAIRS[0], PAIRS[1]):
+                for f in pair:
+                    on_faces((f,), lambda f: halo_copy(it, f ^ 1).wait_recv())
+                    whole = prod[it, f] + halo[it, f] if f < 6 else prod[it, f]
+                    res[f] = loads_v[f].astype(F32) - whole
+                f = pair[0]
+                part = rows_dot(
+                    modes_s[:, f * block : (f + 2) * block], res[f : f + 2].reshape(2 * block, -1)
+                )
+                coarse = part if coarse is None else coarse + part
+        else:
+            for j in range(8):
+                local[j * block : (j + 1) * block, :] = solb[perm[j]]
+            right = local[...]
+            own = None
+            for p, pair in enumerate(PAIRS):
+                rows = op_f[pair[0] * block : (pair[0] + 2) * block, :]
+                both = dot(rows, right)
+                prod[it, pair[0]] = both[:block]
+                prod[it, pair[1]] = both[block:]
+                got = rows_dot(pair_s[p, : 3 * n * (3 if pair[0] < 6 else 1)], both)
+                if pair[0] < 6:
+                    kb_send[pair[0]] = got[n : 2 * n]
+                    kb_send[pair[1]] = got[2 * n :]
+                    on_faces(pair, lambda f: kb_copy(f).start())
+                own = got[:n] if own is None else own + got[:n]
+            on_faces((2, 3, 0, 1), lambda f: halo_copy(it, f).start())
+            coarse = loads_c - own
+            for f in (0, 1, 2, 3, 4, 5):
+                on_faces((f,), lambda f: kb_copy(f ^ 1).wait_recv())
+                coarse = coarse - kb[f]
         c_all[it, gz] = coarse
         t_all[it, gz] = jnp.dot(
             rw_v[...], coarse, precision=HIGH, preferred_element_type=F32
         )
         for off in far_first(nz):
             t_copy(it, off).start()
+        near = sorted({1, nz - 1})
+        for off in near:
+            t_copy(it, off).wait_recv()
         for off in far_first(nz):
             c_copy(it, off).start()
-        if it == 0:
+        if it:
+            on_faces((4, 5), lambda f: halo_copy(it, f).start())
+        else:
             for off in range(1, ny):
                 r_copy(off).wait_recv()
             loaded["rinv"].wait()
@@ -261,7 +283,8 @@
             loaded["root"].wait()
             rinv_s[...] = split_rows(rinv2[...].reshape(rinv_s.shape[0] // 3, -1))
         for off in range(1, nz):
-            t_copy(it, off).wait_recv()
+            if off not in near:
+                t_copy(it, off).wait_recv()
         total = t_all[it, 0]
         for b in range(1, nz):
             total = total + t_all[it, b]
@@ -283,20 +306,48 @@
         rp_all[it, gy] = rp_send[it, gy]
         for off in far_first(ny):
             rp_copy(it, off).start()
-        for f in range(8):
-            old = start_v[f].astype(F32) if it == 0 else sol[f]
+        for f in (6, 7, 0, 1, 2, 3, 4, 5):
+            if it:
+                on_faces((f,), lambda f: halo_copy(it, f ^ 1).wait_recv())
+                whole = prod[it, f] + halo[it, f] if f < 6 else prod[it, f]
+                rest = loads_v[f].astype(F32) - whole
+                old = sol[f]
+            else:
+                rest = res[f]
+                old = start_v[f].astype(F32)
             scale = wb[f]
-            sol[f] = old + jnp.concatenate([scale] * (old.shape[1] // block), axis=1) * res[f]
+            sol[f] = old + jnp.concatenate([scale] * (old.shape[1] // block), axis=1) * rest
+        if it == 0:
+            for f in range(8):
+                op_f[f * block : (f + 1) * block, :] = op_v[inverse[f]]
+            for f in range(8):
+                got = dot(modes_s[:, f * block : (f + 1) * block], loads_v[f])
+                loads_c = got if loads_c is None else loads_c + got
+            loads_c = (loads_c[2 * n :] + loads_c[n : 2 * n]) + loads_c[:n]
+            pair_s[3, : 3 * n] = modes_s[:, 6 * block :]
+            fill = jnp.zeros((n, block), F32)
+            for p in range(3):
+                pair = PAIRS[p]
+                on_faces(pair, lambda f: modes_copy(f ^ 1).wait_recv())
+                pair_s[p] = split_rows(
+                    jnp.concatenate([
+                        modes_v[:, pair[0] * block : (pair[0] + 2) * block],
+                        jnp.concatenate([nbm[pair[0]], fill], axis=1),
+                        jnp.concatenate([fill, nbm[pair[1]]], axis=1),
+                    ], axis=0)
+                )
         for off in range(1, ny):
             rp_copy(it, off).wait_recv()
         region = rp_all[it, 0]
         for a in range(1, ny):
             region = region + rp_all[it, a]
         depth = modes_t.shape[1]
-        sol[...] = sol[...] + dot(modes_t[...], deep_right(region, depth)).reshape(sol.shape)
-        if it == ITERS - 1:
-            base_out = pltpu.make_async_copy(sol, base_o, out_sem.at[1])
-            base_out.start()
+        with_region = sol[...] + dot(modes_t[...], deep_right(region, depth)).reshape(sol.shape)
+        if it < ITERS - 1:
+            sol[...] = with_region
+        else:
+            base_o[...] = with_region
+            g_o[...] = g_t[...]
         for off in range(1, nchip):
             z_copy(it, off).wait_recv()
         stack = z_all[it].reshape(nx * z_all.shape[2], -1)
@@ -312,17 +363,12 @@
             sol[...] = new
             solb[...] = new.astype(BF16)
         else:
-            root_v[...] = root
-
-    root_out = pltpu.make_async_copy(root_v, root_o, out_sem.at[2])
-    root_out.start()
+            root_o[...] = root
+
+    on_faces(range(6), lambda f: modes_copy(f).wait_send())
+    on_faces(range(6), lambda f: kb_copy(f).wait_send())
     for it in range(ITERS):
-        for f in range(6):
-
-            @pl.when(has[f])
-            def _(it=it, f=f):
-                halo_copy(it, f).wait_send()
-
+        on_faces(range(6), lambda f: halo_copy(it, f).wait_send())
         for off in range(1, nz):
             t_copy(it, off).wait_send()
             c_copy(it, off).wait_send()
@@ -335,13 +381,19 @@
     for off in range(1, ny):
         r_copy(off).wait_send()
     root_copy.wait_send()
-    g_out.wait()
-    base_out.wait()
-    root_out.wait()
-
-
-def last_update(base, g, root, out):
-    out[...] = base[...] + dot(g[...], deep_right(root[...], g.shape[1]))
+
+
+def last_update(base, g, root, out_h, out, sem):
+    right = deep_right(root[...], g.shape[1])
+    steps, rows = out.shape[0], out.shape[1]
+    sent = []
+    for i in range(steps):
+        at = slice(i * rows, (i + 1) * rows)
+        out[i] = base[at] + dot(g[at], right)
+        sent.append(pltpu.make_async_copy(out.at[i], out_h.at[i], sem.at[i]))
+        sent[-1].start()
+    for copy in sent:
+        copy.wait()
 
 
 def per_device(
@@ -355,7 +407,8 @@
     width = nz * modes_n
     faces = (8, block, cases)
     deep_m, deep_g = pad_to(6 * modes_n, 128), pad_to(6 * rm, 128)
-    any_spec = pl.BlockSpec(memory_space=pltpu.HBM)
+    hbm_spec = pl.BlockSpec(memory_space=pltpu.HBM)
+    vmem_spec = pl.BlockSpec(memory_space=pltpu.VMEM)
     dma = pltpu.SemaphoreType.DMA
     base, g, root = pl.pallas_call(
         functools.partial(kernel, nx, ny, nz),
@@ -364,12 +417,14 @@
             jax.ShapeDtypeStruct((iface, deep_g), BF16),
             jax.ShapeDtypeStruct((rm, cases), F32),
         ),
-        in_specs=[pl.BlockSpec(memory_space=pltpu.SMEM)] + [any_spec] * 8,
-        out_specs=(any_spec,) * 3,
+        in_specs=[hbm_spec] * 9,
+        out_specs=(vmem_spec,) * 3,
         scratch_shapes=[
+            pltpu.SMEM((8,), jnp.int32),
             pltpu.VMEM(faces, BF16),
             pltpu.VMEM(faces, BF16),
             pltpu.VMEM((8, block, iface), BF16),
+            pltpu.VMEM((iface, iface), BF16),
             pltpu.VMEM((8, block), F32),
             pltpu.VMEM((modes_n, iface), F32),
             pltpu.VMEM((rm, modes_n), F32),
@@ -381,12 +436,16 @@
             pltpu.VMEM(faces, F32),
             pltpu.VMEM((8, block, block), F32),
             pltpu.VMEM((3 * modes_n, iface), BF16),
+            pltpu.VMEM((4, 9 * modes_n, 2 * block), BF16),
             pltpu.VMEM((iface, deep_m), BF16),
             pltpu.VMEM((iface, deep_g), BF16),
+            pltpu.VMEM((6, modes_n, block), F32),
             pltpu.VMEM((ny, modes_n, width), F32),
             pltpu.VMEM((3 * ny * modes_n, width), BF16),
             pltpu.VMEM((2, rm, nx * rm), F32),
             pltpu.VMEM((6 * rm, nx * rm), BF16),
+            pltpu.VMEM((6, modes_n, cases), F32),
+            pltpu.VMEM((6, modes_n, cases), F32),
             pltpu.VMEM((ITERS, nz, rm, cases), F32),
             pltpu.VMEM((ITERS, nz, modes_n, cases), F32),
             pltpu.VMEM((ITERS, ny, rm, cases), F32),
@@ -395,9 +454,10 @@
             pltpu.VMEM((ITERS, nx, rm, cases), F32),
             pltpu.VMEM((ITERS, rm, cases), F32),
             pltpu.VMEM((ITERS, rm, cases), F32),
-            pltpu.VMEM((rm, cases), F32),
-            dma((8,)),
+            dma((9,)),
             dma((ITERS, 6)), dma((ITERS, 6)),
+            dma((6,)), dma((6,)),
+            dma((6,)), dma((6,)),
             dma((ITERS, nz)), dma((ITERS, nz)),
             dma((ITERS, nz)), dma((ITERS, nz)),
             dma((ITERS, ny)), dma((ITERS, ny)),
@@ -406,34 +466,35 @@
             dma((ITERS, ny)), dma((ITERS, ny)),
             dma((ITERS,)), dma((ITERS,)),
             dma(()), dma(()),
-            dma((3,)),
         ],
         compiler_params=pltpu.CompilerParams(
-            collective_id=0, has_side_effects=True, vmem_limit_bytes=67043328
+            collective_id=0, has_side_effects=True, vmem_limit_bytes=44 * 2**20
         ),
         name="iterate",
     )(
-        block_order.reshape(8),
-        loads.reshape(faces),
-        start.reshape(faces),
-        interface_op.reshape(8, block, iface),
-        interface_weights.reshape(8, block),
-        coarse_modes.reshape(modes_n, iface),
-        region_weights.reshape(modes_n, rm).T,
-        region_inverse.reshape(modes_n, -1),
-        root_inverse,
+        *(
+            pltpu.with_memory_space_constraint(x, pltpu.HBM)
+            for x in (
+                block_order.reshape(8),
+                loads.reshape(faces),
+                start.reshape(faces),
+                interface_op.reshape(8, block, iface),
+                interface_weights.reshape(8, block),
+                coarse_modes.reshape(modes_n, iface),
+                region_weights.reshape(modes_n, rm).T,
+                region_inverse.reshape(modes_n, -1),
+                root_inverse,
+            )
+        )
     )
-    steps = 4
+    rows = (4, iface // 4, cases)
     out = pl.pallas_call(
         last_update,
-        grid=(steps,),
-        out_shape=jax.ShapeDtypeStruct((iface, cases), F32),
-        in_specs=[
-            pl.BlockSpec((iface // steps, cases), lambda i: (i, 0)),
-            pl.BlockSpec((iface // steps, deep_g), lambda i: (i, 0)),
-            pl.BlockSpec((rm, cases), lambda i: (0, 0)),
-        ],
-        out_specs=pl.BlockSpec((iface // steps, cases), lambda i: (i, 0)),
+        out_shape=jax.ShapeDtypeStruct(rows, F32),
+        in_specs=[vmem_spec] * 3,
+        out_specs=hbm_spec,
+        scratch_shapes=[pltpu.VMEM(rows, F32), dma((4,))],
+        compiler_params=pltpu.CompilerParams(vmem_limit_bytes=16 * 2**20),
         name="last_update",
     )(base.reshape(iface, cases), g, root)
     return out.reshape(1, 1, 1, iface, cases)

time: 76 us -> 69.9 us (0.920)
  Pallas kernels: 75.8 us -> 69.7 us
    pallas_call x1, Pallas kernels: 72.1 us -> 68.5 us  [per_device(): pl.pallas_call(functools.partial(kernel, nx, ny, nz), out_shape=(jax.Shap...]
    pallas_call x1, Pallas kernels: 3.69 us -> 1.22 us  [per_device(): pl.pallas_call(last_update, out_shape=jax.ShapeDtypeStruct(rows, F32), in...]
where the time goes in v3:
time: 69.9 us; the launch traced here: 69.8 us
  Pallas kernels  69.7 us (100%)
    pallas_call x1, Pallas kernels, per_device(): pl.pallas_call(functools.partial(kernel, nx, ny, nz), out_shape=(jax.Shap...  68.5 us

profile of v3, /device:TPU:1, one launch (start us, length us, event | category | flops | bytes accessed | tf_op | source)
XLA Modules:
  0.0 69.8 jit_solution(9378775792905834640)
XLA Ops:
  0.0 68.5 %iterate.1 = (f32[8,128,256]{2,1,0:T(8,128)S(1)}, bf16[1024,128]{1,0:T(8,128)(2,1)S(1)}, f32[16,256]{1,0:T(8,128)S(1)}) custom-call(s32[8]{0:T(128)} %bitcast.20, bf16[8,128,256]{2,1,0:T(8,128)(2,1)} %bitcast.14, bf16[8,128,256]{2,1,0:T(8,128)(2,1)} %bitcast.15, bf16[8,128,1024]{2,1,0:T(8,128)(2,1)} %bitcast.13, f32[8,128]{1,0:T(8,128)} %bitcast.19, ...), custom_call_target="tpu_custom_call" | custom-call | tf_op jit(solution)/shard_map/iterate/pallas_call | solution.py:413
  68.5 1.2 %last_update.1 = f32[4,256,256]{2,1,0:T(8,128)} custom-call(f32[1024,256]{1,0:T(8,128)S(1)} %bitcast.12, bf16[1024,128]{1,0:T(8,128)(2,1)S(1)} %get-tuple-element.9.g, f32[16,256]{1,0:T(8,128)S(1)} %get-tuple-element.10.root), custom_call_target="tpu_custom_call" | custom-call | tf_op jit(solution)/shard_map/last_update/pallas_call | solution.py:491

commit v4 on v3

--- a/solution.py
+++ b/solution.py
@@ -67,7 +67,7 @@
     nx, ny, nz,
     perm_h, loads_h, start_h, op_h, w_h, modes_h, rw_h, rinv_h, root_h,
     base_o, g_o, root_o,
-    perm_s, loads_v, start_v, op_v, op_f, w_v, modes_v, rw_v,
+    perm_s, loads_v, start_v, op_v, op_f, w_v, modes_v, rw_v, rinv_v, r_send,
     local, prod, halo, sol, solb, res, wb, modes_s, pair_s, modes_t, g_t, nbm,
     rblk, rblk_s, rinv2, rinv_s, kb_send, kb,
     t_all, c_all, s_all, rp_send, rp_all, z_all, p_send, p_recv,
@@ -100,14 +100,11 @@
             device_id=device, device_id_type=MESH,
         )
 
-    def columns(a):
-        return pl.ds(pl.multiple_of(a * width, 128), width)
-
     loaded = {}
     for i, (name, src, dst) in enumerate((
         ("perm", perm_h, perm_s), ("start", start_h, start_v), ("op", op_h, op_v), ("modes", modes_h, modes_v), ("rw", rw_h, rw_v),
         ("loads", loads_h, loads_v), ("w", w_h, w_v), ("root", root_h, rinv2.at[0]),
-        ("rinv", rinv_h.at[:, columns(gy)], rblk.at[gy]),
+        ("rinv", rinv_h, rinv_v),
     )):
         loaded[name] = pltpu.make_async_copy(src, dst, in_sem.at[i])
         loaded[name].start()
@@ -171,7 +168,7 @@
 
     def c_copy(it, off):
         return remote(
-            c_all.at[it, gz], c_all.at[it, gz], cs.at[it, off], cr.at[it, off], along_z(off)
+            c_all.at[it, gy], c_all.at[it, gy], cs.at[it, off], cr.at[it, off], along_y(off)
         )
 
     def s_copy(it, off):
@@ -185,13 +182,13 @@
         )
 
     def r_copy(off):
-        to = along_y(off)
-        return remote(rinv_h.at[:, columns(to[1])], rblk.at[gy], rs.at[off], rr.at[off], to)
+        to = along_z(off)
+        return remote(r_send.at[to[2]], rblk.at[gz], rs.at[off], rr.at[off], to)
 
     def rp_copy(it, off):
-        to = along_y(off)
+        to = along_z(off)
         return remote(
-            rp_send.at[it, to[1]], rp_all.at[it, gy], ps.at[it, off], pr.at[it, off], to
+            rp_send.at[it, to[2]], rp_all.at[it, gz], ps.at[it, off], pr.at[it, off], to
         )
 
     def m_copy(it):
@@ -214,8 +211,18 @@
             on_faces(FACES, lambda f: halo_copy(it, f).start())
             on_faces(range(6), lambda f: modes_copy(f).start())
             root_copy.start()
-            for off in range(1, ny):
+            loaded["rinv"].wait()
+            for b in range(nz):
+                r_send[b] = jnp.concatenate(
+                    [
+                        rinv_v[:, a * width + b * n : a * width + (b + 1) * n]
+                        for a in range(ny)
+                    ],
+                    axis=1,
+                )
+            for off in far_first(nz):
                 r_copy(off).start()
+            rblk[gz] = r_send[gz]
             loaded["modes"].wait()
             loaded["loads"].wait()
             loaded["rw"].wait()
@@ -256,41 +263,45 @@
                     kb_send[pair[1]] = got[2 * n :]
                     on_faces(pair, lambda f: kb_copy(f).start())
                 own = got[:n] if own is None else own + got[:n]
-            on_faces((2, 3, 0, 1), lambda f: halo_copy(it, f).start())
+            on_faces((0, 1), lambda f: halo_copy(it, f).start())
             coarse = loads_c - own
             for f in (0, 1, 2, 3, 4, 5):
                 on_faces((f,), lambda f: kb_copy(f ^ 1).wait_recv())
                 coarse = coarse - kb[f]
-        c_all[it, gz] = coarse
+        c_all[it, gy] = coarse
         t_all[it, gz] = jnp.dot(
             rw_v[...], coarse, precision=HIGH, preferred_element_type=F32
         )
         for off in far_first(nz):
             t_copy(it, off).start()
-        near = sorted({1, nz - 1})
-        for off in near:
-            t_copy(it, off).wait_recv()
-        for off in far_first(nz):
+        for off in far_first(ny):
             c_copy(it, off).start()
         if it:
-            on_faces((4, 5), lambda f: halo_copy(it, f).start())
+            on_faces((2, 3), lambda f: halo_copy(it, f).start())
         else:
-            for off in range(1, ny):
+            for off in range(1, nz):
                 r_copy(off).wait_recv()
-            loaded["rinv"].wait()
             rblk_s[...] = split_rows(rblk[...].reshape(rblk_s.shape[0] // 3, -1))
             root_copy.wait_recv()
             loaded["root"].wait()
             rinv_s[...] = split_rows(rinv2[...].reshape(rinv_s.shape[0] // 3, -1))
+        for off in range(1, ny):
+            c_copy(it, off).wait_recv()
+        part = rows_dot(rblk_s[...], c_all[it].reshape(ny * n, -1))
+        rp_send[it] = part.reshape(rp_send.shape[1:])
         for off in range(1, nz):
-            if off not in near:
-                t_copy(it, off).wait_recv()
+            t_copy(it, off).wait_recv()
         total = t_all[it, 0]
         for b in range(1, nz):
             total = total + t_all[it, b]
         s_all[it, gy] = total
         for off in far_first(ny):
             s_copy(it, off).start()
+        for off in far_first(nz):
+            rp_copy(it, off).start()
+        rp_all[it, gz] = rp_send[it, gz]
+        if it:
+            on_faces((4, 5), lambda f: halo_copy(it, f).start())
         for off in range(1, ny):
             s_copy(it, off).wait_recv()
         total = s_all[it, 0]
@@ -299,13 +310,6 @@
         z_all[it, gx] = total
         for off in far_first(nchip):
             z_copy(it, off).start()
-        for off in range(1, nz):
-            c_copy(it, off).wait_recv()
-        part = rows_dot(rblk_s[...], c_all[it].reshape(width, -1))
-        rp_send[it] = part.reshape(rp_send.shape[1:])
-        rp_all[it, gy] = rp_send[it, gy]
-        for off in far_first(ny):
-            rp_copy(it, off).start()
         for f in (6, 7, 0, 1, 2, 3, 4, 5):
             if it:
                 on_faces((f,), lambda f: halo_copy(it, f ^ 1).wait_recv())
@@ -336,11 +340,11 @@
                         jnp.concatenate([fill, nbm[pair[1]]], axis=1),
                     ], axis=0)
                 )
-        for off in range(1, ny):
+        for off in range(1, nz):
             rp_copy(it, off).wait_recv()
         region = rp_all[it, 0]
-        for a in range(1, ny):
-            region = region + rp_all[it, a]
+        for b in range(1, nz):
+            region = region + rp_all[it, b]
         depth = modes_t.shape[1]
         with_region = sol[...] + dot(modes_t[...], deep_right(region, depth)).reshape(sol.shape)
         if it < ITERS - 1:
@@ -371,14 +375,14 @@
         on_faces(range(6), lambda f: halo_copy(it, f).wait_send())
         for off in range(1, nz):
             t_copy(it, off).wait_send()
-            c_copy(it, off).wait_send()
+            rp_copy(it, off).wait_send()
         for off in range(1, ny):
             s_copy(it, off).wait_send()
-            rp_copy(it, off).wait_send()
+            c_copy(it, off).wait_send()
         for off in range(1, nchip):
             z_copy(it, off).wait_send()
         m_copy(it).wait_send()
-    for off in range(1, ny):
+    for off in range(1, nz):
         r_copy(off).wait_send()
     root_copy.wait_send()
 
@@ -428,6 +432,8 @@
             pltpu.VMEM((8, block), F32),
             pltpu.VMEM((modes_n, iface), F32),
             pltpu.VMEM((rm, modes_n), F32),
+            pltpu.VMEM((modes_n, ny * width), F32),
+            pltpu.VMEM((nz, modes_n, ny * modes_n), F32),
             pltpu.VMEM((iface, cases), BF16),
             pltpu.VMEM((ITERS, *faces), F32),
             pltpu.VMEM((ITERS, 6, block, cases), F32),
@@ -440,17 +446,17 @@
             pltpu.VMEM((iface, deep_m), BF16),
             pltpu.VMEM((iface, deep_g), BF16),
             pltpu.VMEM((6, modes_n, block), F32),
-            pltpu.VMEM((ny, modes_n, width), F32),
-            pltpu.VMEM((3 * ny * modes_n, width), BF16),
+            pltpu.VMEM((nz, modes_n, ny * modes_n), F32),
+            pltpu.VMEM((3 * width, ny * modes_n), BF16),
             pltpu.VMEM((2, rm, nx * rm), F32),
             pltpu.VMEM((6 * rm, nx * rm), BF16),
             pltpu.VMEM((6, modes_n, cases), F32),
             pltpu.VMEM((6, modes_n, cases), F32),
             pltpu.VMEM((ITERS, nz, rm, cases), F32),
+            pltpu.VMEM((ITERS, ny, modes_n, cases), F32),
+            pltpu.VMEM((ITERS, ny, rm, cases), F32),
             pltpu.VMEM((ITERS, nz, modes_n, cases), F32),
-            pltpu.VMEM((ITERS, ny, rm, cases), F32),
-            pltpu.VMEM((ITERS, ny, modes_n, cases), F32),
-            pltpu.VMEM((ITERS, ny, modes_n, cases), F32),
+            pltpu.VMEM((ITERS, nz, modes_n, cases), F32),
             pltpu.VMEM((ITERS, nx, rm, cases), F32),
             pltpu.VMEM((ITERS, rm, cases), F32),
             pltpu.VMEM((ITERS, rm, cases), F32),
@@ -459,11 +465,11 @@
             dma((6,)), dma((6,)),
             dma((6,)), dma((6,)),
             dma((ITERS, nz)), dma((ITERS, nz)),
-            dma((ITERS, nz)), dma((ITERS, nz)),
+            dma((ITERS, ny)), dma((ITERS, ny)),
             dma((ITERS, ny)), dma((ITERS, ny)),
             dma((ITERS, nchip)), dma((ITERS, nchip)),
-            dma((ny,)), dma((ny,)),
-            dma((ITERS, ny)), dma((ITERS, ny)),
+            dma((nz,)), dma((nz,)),
+            dma((ITERS, nz)), dma((ITERS, nz)),
             dma((ITERS,)), dma((ITERS,)),
             dma(()), dma(()),
         ],

time: 69.9 us -> 69.8 us (level)
  no operation moved by 1% of the time
where the time goes in v4:
time: 69.8 us; the launch traced here: 69.7 us
  Pallas kernels  69.7 us (100%)
    pallas_call x1, Pallas kernels, per_device(): pl.pallas_call(functools.partial(kernel, nx, ny, nz), out_shape=(jax.Shap...  68.5 us

profile of v4, /device:TPU:1, one launch (start us, length us, event | category | flops | bytes accessed | tf_op | source)
XLA Modules:
  0.0 69.7 jit_solution(8555439251097734967)
XLA Ops:
  0.0 68.5 %iterate.1 = (f32[8,128,256]{2,1,0:T(8,128)S(1)}, bf16[1024,128]{1,0:T(8,128)(2,1)S(1)}, f32[16,256]{1,0:T(8,128)S(1)}) custom-call(s32[8]{0:T(128)} %bitcast.20, bf16[8,128,256]{2,1,0:T(8,128)(2,1)} %bitcast.14, bf16[8,128,256]{2,1,0:T(8,128)(2,1)} %bitcast.15, bf16[8,128,1024]{2,1,0:T(8,128)(2,1)} %bitcast.13, f32[8,128]{1,0:T(8,128)} %bitcast.19, ...), custom_call_target="tpu_custom_call" | custom-call | tf_op jit(solution)/shard_map/iterate/pallas_call | solution.py:417
  68.5 1.2 %last_update.1 = f32[4,256,256]{2,1,0:T(8,128)} custom-call(f32[1024,256]{1,0:T(8,128)S(1)} %bitcast.12, bf16[1024,128]{1,0:T(8,128)(2,1)S(1)} %get-tuple-element.9.g, f32[16,256]{1,0:T(8,128)S(1)} %get-tuple-element.10.root), custom_call_target="tpu_custom_call" | custom-call | tf_op jit(solution)/shard_map/last_update/pallas_call | solution.py:497

commit v5 on v4

--- a/solution.py
+++ b/solution.py
@@ -39,6 +39,13 @@
     q = dot(left[: 2 * n], mid)
     r = dot(left[:n], low)
     return ((r + q[n:]) + p[2 * n :]) + (q[:n] + p[n : 2 * n]) + p[:n]
+
+
+def rows_dot_last(left, right):
+    n = left.shape[0] // 3
+    high = right.astype(BF16)
+    p = dot(left[: 2 * n], high)
+    return (dot(left[:n], (right - high.astype(F32)).astype(BF16)) + p[n:]) + p[:n]
 
 
 def deep_left(x, depth):
@@ -71,7 +78,7 @@
     local, prod, halo, sol, solb, res, wb, modes_s, pair_s, modes_t, g_t, nbm,
     rblk, rblk_s, rinv2, rinv_s, kb_send, kb,
     t_all, c_all, s_all, rp_send, rp_all, z_all, p_send, p_recv,
-    in_sem, hs, hr, ns, nr, ks, kr, ts, tr, cs, cr, ss, sr, zs, zr, rs, rr, ps, pr, ms, mr, xs, xr,
+    in_sem, hs, hr, ns, nr, ks, kr, ts, tr, cs, cr, ss, sr, zs, zr, rs, rr, ps, pr, ms, mr, xs, xr, root_v, out_sem,
 ):
     gx, gy, gz = lax.axis_index("gx"), lax.axis_index("gy"), lax.axis_index("gz")
     nchip = nx // 2
@@ -100,6 +107,14 @@
             device_id=device, device_id_type=MESH,
         )
 
+    barrier = pltpu.get_barrier_semaphore()
+    greeted = (
+        [along_x(o) for o in far_first(nchip)] + [along_z(o) for o in far_first(nz)]
+        + [along_y(o) for o in far_first(ny)] + [beside, mate]
+    )
+    for device in greeted:
+        pl.semaphore_signal(barrier, inc=1, device_id=device, device_id_type=MESH)
+
     loaded = {}
     for i, (name, src, dst) in enumerate((
         ("perm", perm_h, perm_s), ("start", start_h, start_v), ("op", op_h, op_v), ("modes", modes_h, modes_v), ("rw", rw_h, rw_v),
@@ -109,14 +124,6 @@
         loaded[name] = pltpu.make_async_copy(src, dst, in_sem.at[i])
         loaded[name].start()
 
-    barrier = pltpu.get_barrier_semaphore()
-    greeted = (
-        [along_x(o) for o in far_first(nchip)] + [along_z(o) for o in far_first(nz)]
-        + [along_y(o) for o in far_first(ny)] + [beside, mate]
-    )
-    for device in greeted:
-        pl.semaphore_signal(barrier, inc=1, device_id=device, device_id_type=MESH)
-
     has = (gx > 0, gx < nx - 1, gy > 0, gy < ny - 1, gz > 0, gz < nz - 1)
     towards = (
         (lax.rem(gx + nx - 1, nx), gy, gz), (lax.rem(gx + 1, nx), gy, gz),
@@ -127,15 +134,6 @@
         return remote(
             prod.at[it, f], halo.at[it, f ^ 1], hs.at[it, f], hr.at[it, f ^ 1], towards[f]
         )
-
-    for f in range(6):
-
-        @pl.when(jnp.logical_not(has[f]))
-        def _(f=f):
-            nbm[f] = jnp.zeros_like(nbm[f])
-            kb[f] = jnp.zeros_like(kb[f])
-            for it in range(ITERS):
-                halo[it, f] = jnp.zeros_like(halo[it, f])
 
     loaded["perm"].wait()
     perm = [perm_s[j] for j in range(8)]
@@ -163,32 +161,36 @@
 
     def t_copy(it, off):
         return remote(
-            t_all.at[it, gz], t_all.at[it, gz], ts.at[it, off], tr.at[it, off], along_z(off)
+            t_all.at[it, gz], t_all.at[it, gz], ts.at[it], tr.at[it], along_z(off)
         )
 
     def c_copy(it, off):
         return remote(
-            c_all.at[it, gy], c_all.at[it, gy], cs.at[it, off], cr.at[it, off], along_y(off)
-        )
+            c_all.at[it, gy], c_all.at[it, gy], cs.at[it], cr.at[it], along_y(off)
+        )
+
+    def all_of(buffer, count, sem):
+        blocks = buffer.at[0:count]
+        pltpu.make_async_copy(blocks, blocks, sem).wait()
 
     def s_copy(it, off):
         return remote(
-            s_all.at[it, gy], s_all.at[it, gy], ss.at[it, off], sr.at[it, off], along_y(off)
+            s_all.at[it, gy], s_all.at[it, gy], ss.at[it], sr.at[it], along_y(off)
         )
 
     def z_copy(it, off):
         return remote(
-            z_all.at[it, gx], z_all.at[it, gx], zs.at[it, off], zr.at[it, off], along_x(off)
+            z_all.at[it, gx], z_all.at[it, gx], zs.at[it], zr.at[it], along_x(off)
         )
 
     def r_copy(off):
         to = along_z(off)
-        return remote(r_send.at[to[2]], rblk.at[gz], rs.at[off], rr.at[off], to)
+        return remote(r_send.at[to[2]], rblk.at[gz], rs, rr, to)
 
     def rp_copy(it, off):
         to = along_z(off)
         return remote(
-            rp_send.at[it, to[2]], rp_all.at[it, gz], ps.at[it, off], pr.at[it, off], to
+            rp_send.at[it, to[2]], rp_all.at[it, gz], ps.at[it], pr.at[it], to
         )
 
     def m_copy(it):
@@ -223,6 +225,14 @@
             for off in far_first(nz):
                 r_copy(off).start()
             rblk[gz] = r_send[gz]
+            for f in range(6):
+
+                @pl.when(jnp.logical_not(has[f]))
+                def _(f=f):
+                    nbm[f] = jnp.zeros_like(nbm[f])
+                    kb[f] = jnp.zeros_like(kb[f])
+                    for it in range(ITERS):
+                        halo[it, f] = jnp.zeros_like(halo[it, f])
             loaded["modes"].wait()
             loaded["loads"].wait()
             loaded["rw"].wait()
@@ -257,7 +267,7 @@
                 both = dot(rows, right)
                 prod[it, pair[0]] = both[:block]
                 prod[it, pair[1]] = both[block:]
-                got = rows_dot(pair_s[p, : 3 * n * (3 if pair[0] < 6 else 1)], both)
+                got = rows_dot_last(pair_s[p, : 3 * n * (3 if pair[0] < 6 else 1)], both)
                 if pair[0] < 6:
                     kb_send[pair[0]] = got[n : 2 * n]
                     kb_send[pair[1]] = got[2 * n :]
@@ -279,18 +289,15 @@
         if it:
             on_faces((2, 3), lambda f: halo_copy(it, f).start())
         else:
-            for off in range(1, nz):
-                r_copy(off).wait_recv()
+            all_of(rblk, nz - 1, rr)
             rblk_s[...] = split_rows(rblk[...].reshape(rblk_s.shape[0] // 3, -1))
             root_copy.wait_recv()
             loaded["root"].wait()
             rinv_s[...] = split_rows(rinv2[...].reshape(rinv_s.shape[0] // 3, -1))
-        for off in range(1, ny):
-            c_copy(it, off).wait_recv()
-        part = rows_dot(rblk_s[...], c_all[it].reshape(ny * n, -1))
+        all_of(c_all.at[it], ny - 1, cr.at[it])
+        part = (rows_dot_last if it else rows_dot)(rblk_s[...], c_all[it].reshape(ny * n, -1))
         rp_send[it] = part.reshape(rp_send.shape[1:])
-        for off in range(1, nz):
-            t_copy(it, off).wait_recv()
+        all_of(t_all.at[it], nz - 1, tr.at[it])
         total = t_all[it, 0]
         for b in range(1, nz):
             total = total + t_all[it, b]
@@ -302,8 +309,7 @@
         rp_all[it, gz] = rp_send[it, gz]
         if it:
             on_faces((4, 5), lambda f: halo_copy(it, f).start())
-        for off in range(1, ny):
-            s_copy(it, off).wait_recv()
+        all_of(s_all.at[it], ny - 1, sr.at[it])
         total = s_all[it, 0]
         for a in range(1, ny):
             total = total + s_all[it, a]
@@ -340,25 +346,37 @@
                         jnp.concatenate([fill, nbm[pair[1]]], axis=1),
                     ], axis=0)
                 )
-        for off in range(1, nz):
-            rp_copy(it, off).wait_recv()
+        all_of(rp_all.at[it], nz - 1, pr.at[it])
         region = rp_all[it, 0]
         for b in range(1, nz):
             region = region + rp_all[it, b]
         depth = modes_t.shape[1]
         with_region = sol[...] + dot(modes_t[...], deep_right(region, depth)).reshape(sol.shape)
-        if it < ITERS - 1:
-            sol[...] = with_region
+        sol[...] = with_region
+        if it == ITERS - 1:
+            base_out = pltpu.make_async_copy(sol, base_o, out_sem.at[0])
+            base_out.start()
+            g_out = pltpu.make_async_copy(g_t, g_o, out_sem.at[1])
+            g_out.start()
+        if it == 0:
+            on_faces(range(6), lambda f: modes_copy(f).wait_send())
+            all_of(rblk, nz - 1, rs)
+            root_copy.wait_send()
         else:
-            base_o[...] = with_region
-            g_o[...] = g_t[...]
-        for off in range(1, nchip):
-            z_copy(it, off).wait_recv()
+            on_faces(range(6), lambda f: kb_copy(f).wait_send())
+            m_copy(it - 1).wait_send()
+        on_faces(range(6), lambda f: halo_copy(it, f).wait_send())
+        all_of(t_all.at[it], nz - 1, ts.at[it])
+        all_of(rp_all.at[it], nz - 1, ps.at[it])
+        all_of(s_all.at[it], ny - 1, ss.at[it])
+        all_of(c_all.at[it], ny - 1, cs.at[it])
+        all_of(z_all.at[it], nchip - 1, zr.at[it])
         stack = z_all[it].reshape(nx * z_all.shape[2], -1)
-        both = rows_dot(rinv_s[...], stack)
+        both = (rows_dot_last if it else rows_dot)(rinv_s[...], stack)
         rm = both.shape[0] // 2
         p_send[it] = both[rm:]
         m_copy(it).start()
+        all_of(z_all.at[it], nchip - 1, zs.at[it])
         m_copy(it).wait_recv()
         root = both[:rm] + p_recv[it]
         if it < ITERS - 1:
@@ -367,24 +385,14 @@
             sol[...] = new
             solb[...] = new.astype(BF16)
         else:
-            root_o[...] = root
-
-    on_faces(range(6), lambda f: modes_copy(f).wait_send())
-    on_faces(range(6), lambda f: kb_copy(f).wait_send())
-    for it in range(ITERS):
-        on_faces(range(6), lambda f: halo_copy(it, f).wait_send())
-        for off in range(1, nz):
-            t_copy(it, off).wait_send()
-            rp_copy(it, off).wait_send()
-        for off in range(1, ny):
-            s_copy(it, off).wait_send()
-            c_copy(it, off).wait_send()
-        for off in range(1, nchip):
-            z_copy(it, off).wait_send()
-        m_copy(it).wait_send()
-    for off in range(1, nz):
-        r_copy(off).wait_send()
-    root_copy.wait_send()
+            root_v[...] = root
+            root_out = pltpu.make_async_copy(root_v, root_o, out_sem.at[2])
+            root_out.start()
+
+    m_copy(ITERS - 1).wait_send()
+    base_out.wait()
+    g_out.wait()
+    root_out.wait()
 
 
 def last_update(base, g, root, out_h, out, sem):
@@ -422,7 +430,7 @@
             jax.ShapeDtypeStruct((rm, cases), F32),
         ),
         in_specs=[hbm_spec] * 9,
-        out_specs=(vmem_spec,) * 3,
+        out_specs=(hbm_spec,) * 3,
         scratch_shapes=[
             pltpu.SMEM((8,), jnp.int32),
             pltpu.VMEM(faces, BF16),
@@ -464,14 +472,16 @@
             dma((ITERS, 6)), dma((ITERS, 6)),
             dma((6,)), dma((6,)),
             dma((6,)), dma((6,)),
-            dma((ITERS, nz)), dma((ITERS, nz)),
-            dma((ITERS, ny)), dma((ITERS, ny)),
-            dma((ITERS, ny)), dma((ITERS, ny)),
-            dma((ITERS, nchip)), dma((ITERS, nchip)),
-            dma((nz,)), dma((nz,)),
-            dma((ITERS, nz)), dma((ITERS, nz)),
+            dma((ITERS,)), dma((ITERS,)),
+            dma((ITERS,)), dma((ITERS,)),
+            dma((ITERS,)), dma((ITERS,)),
             dma((ITERS,)), dma((ITERS,)),
             dma(()), dma(()),
+            dma((ITERS,)), dma((ITERS,)),
+            dma((ITERS,)), dma((ITERS,)),
+            dma(()), dma(()),
+            pltpu.VMEM((rm, cases), F32),
+            dma((3,)),
         ],
         compiler_params=pltpu.CompilerParams(
             collective_id=0, has_side_effects=True, vmem_limit_bytes=44 * 2**20

time: 69.8 us -> 68 us (0.974)
  Pallas kernels: 69.7 us -> 67.9 us
    pallas_call x1, Pallas kernels: 68.5 us -> 66.6 us  [per_device(): pl.pallas_call(functools.partial(kernel, nx, ny, nz), out_shape=(jax.Shap...]
where the time goes in v5:
time: 68 us; the launch traced here: 67.9 us
  Pallas kernels  67.9 us (100%)
    pallas_call x1, Pallas kernels, per_device(): pl.pallas_call(functools.partial(kernel, nx, ny, nz), out_shape=(jax.Shap...  66.6 us

profile of v5, /device:TPU:1, one launch (start us, length us, event | category | flops | bytes accessed | tf_op | source)
XLA Modules:
  0.0 67.9 jit_solution(9284606141826639128)
XLA Ops:
  0.0 66.6 %iterate.1 = (f32[8,128,256]{2,1,0:T(8,128)S(1)}, bf16[1024,128]{1,0:T(8,128)(2,1)S(1)}, f32[16,256]{1,0:T(8,128)S(1)}) custom-call(s32[8]{0:T(128)} %bitcast.20, bf16[8,128,256]{2,1,0:T(8,128)(2,1)} %bitcast.14, bf16[8,128,256]{2,1,0:T(8,128)(2,1)} %bitcast.15, bf16[8,128,1024]{2,1,0:T(8,128)(2,1)} %bitcast.13, f32[8,128]{1,0:T(8,128)} %bitcast.19, ...), custom_call_target="tpu_custom_call" | custom-call | tf_op jit(solution)/shard_map/iterate/pallas_call | solution.py:425
  66.6 1.2 %last_update.1 = f32[4,256,256]{2,1,0:T(8,128)} custom-call(f32[1024,256]{1,0:T(8,128)S(1)} %bitcast.12, bf16[1024,128]{1,0:T(8,128)(2,1)S(1)} %get-tuple-element.9.g, f32[16,256]{1,0:T(8,128)S(1)} %get-tuple-element.10.root), custom_call_target="tpu_custom_call" | custom-call | tf_op jit(solution)/shard_map/last_update/pallas_call | solution.py:507
